TPU v7x, 256 devices: a whole 4x4x8 slice. The times are simulated.
256 devices in a mesh: stn: 64 (over z, y, core), band: 4 (over x).
Axes of the slice: x: 4, y: 4, z: 8, core: 2. Of those that a mesh axis runs over, the one named last changes fastest.
Arguments:
- voltages: bfloat16 [2, 512, 1024, 256], P(None, 'band', 'stn'), may hold values from -8 to 8
- group_count: int32 [4, 64], replicated, may hold values from 1 to 4, 128 in all within a row
- levels: int32 [4, 128], replicated, may hold values from 0 to 63
- bandpass: float32 [64], replicated, may hold values from 0.25 to 4
- block_order: int32 [64], replicated, may hold values from 0 to 63, each once
Outputs:
- tile_vis: bfloat16 [64, 64, 4, 2, 128, 128], P('stn', None, None, None, 'band')
Inputs may be any that keep to these rules, and one draw needn't show every extreme that they name: `group_count`: in each band's row the 64 group sizes sum to 128, and the largest is exactly 4. `block_order`: each baseline block stands in exactly one slot.
All inputs are finite; a program needn't handle non-finite values.
Results may differ from a plain program's by a relative error of at most 0.001.
Values may be sent and summed in bfloat16 or wider, within the bound.
No kernel may reach another device: no remote copies, remote signals or barrier semaphores. Data moves between devices by JAX's collectives and lax.ppermute only.
A program may use at most 64 MiB of HBM per device.

v0:
```python
import jax
import jax.numpy as jnp
from jax import lax
from jax.sharding import PartitionSpec as P

SP = 1024
TIME = 256
BB = 128
LEVELS = 64
MOST = 4


def correlate_full(channel):
    right_side = jnp.concatenate([channel[0], channel[1]], axis=1)
    swapped = jnp.concatenate([channel[1], -channel[0]], axis=1)
    stacked = jnp.concatenate([right_side, swapped], axis=0)
    return lax.dot_general(
        stacked, right_side, (((1,), (1,)), ((), ())), preferred_element_type=jnp.float32
    )


def body(voltages, group_count, levels, bandpass, block_order):
    station_count = lax.axis_size("stn")
    my_index = lax.axis_index("stn")
    band_index = lax.axis_index("band")
    ch_band = voltages.shape[1]
    sp_dev = voltages.shape[2]
    samples = voltages.shape[3]
    counts = lax.dynamic_index_in_dim(group_count, band_index, 0, keepdims=False)
    starts = jnp.cumsum(counts) - counts
    slot_ids = jnp.arange(MOST, dtype=jnp.int32)
    picked = jnp.minimum(starts[None, :] + slot_ids[:, None], ch_band - 1).reshape(-1)
    outgoing = jnp.take(voltages, picked, axis=1).reshape(2, MOST, station_count, sp_dev, samples)
    my_size = lax.dynamic_index_in_dim(counts, my_index, 0, keepdims=False)
    my_start = lax.dynamic_index_in_dim(starts, my_index, 0, keepdims=False)
    level_row = lax.dynamic_index_in_dim(levels, band_index, 0, keepdims=False)
    one_hot = (level_row[:, None] == jnp.arange(LEVELS, dtype=jnp.int32)[None, :]).astype(
        jnp.float32
    )
    gain_row = jnp.dot(one_hot, bandpass, precision=lax.Precision.HIGHEST)
    gain_row = jnp.concatenate([gain_row, jnp.zeros((MOST,), jnp.float32)])
    weights = lax.dynamic_slice_in_dim(gain_row, my_start, MOST) / (
        my_size.astype(jnp.float32) * TIME
    )
    block_count = SP // BB

    def correlate(channel):
        flat = channel.reshape(2, SP, samples)
        return correlate_full(flat)

    empty = jnp.zeros((2 * SP, SP), jnp.float32)
    arrived = lax.all_to_all(outgoing, "stn", split_axis=2, concat_axis=2, tiled=True)

    def accumulate(slot, totals):
        channel = lax.dynamic_index_in_dim(arrived, slot, 1, keepdims=False)
        return totals + weights[slot] * correlate(channel)

    totals = lax.fori_loop(jnp.int32(0), my_size, accumulate, empty)
    tiles = totals.reshape(2, block_count, BB, block_count, BB).transpose(1, 3, 0, 2, 4)
    tiles = tiles.reshape(block_count * block_count, 2, BB, BB)
    tiles = tiles.astype(jnp.bfloat16)
    slot_order = block_order.reshape(station_count, -1).T.reshape(-1)
    sending = jnp.take(tiles, slot_order, axis=0).reshape(-1, station_count, 1, 2, BB, BB)
    return lax.all_to_all(
        lax.all_to_all(sending, "stn", split_axis=1, concat_axis=1, tiled=True),
        "band",
        split_axis=4,
        concat_axis=2,
        tiled=True,
    )


def solution(mesh):
    return jax.shard_map(
        body,
        mesh=mesh,
        in_specs=(P(None, "band", "stn", None), P(), P(), P(), P()),
        out_specs=P("stn", None, None, None, "band", None),
        check_vma=False,
    )
```

profile of v0, /device:TPU:32, one launch (start us, length us, event | category | flops | bytes accessed | tf_op | source)
XLA Modules:
  0.0 370.3 jit_solution(3243247778791661921)
XLA Ops:
  0.0 0.0 copy-start
  0.0 0.8 fusion.16
  0.8 0.1 copy.30
  0.9 0.1 reduce-window.4
  1.0 0.1 reduce.1
  1.1 0.7 fusion.14
  1.9 0.1 min.22
  2.0 0.0 copy-done
  2.0 2.8 gather_fusion
  4.8 2.5 copy.31
  7.3 0.7 broadcast_select_fusion
  8.0 2.7 copy.32
  10.7 0.0 copy-start.2
  10.7 0.0 copy-start.3
  10.7 0.0 copy-start.4
  10.7 12.1 %all-to-all-start = ((bf16[2,4,64,16,256]{4,3,1,0,2:T(8,128)(2,1)}), bf16[2,4,64,16,256]{4,3,1,0,2:T(8,128)(2,1)}, u32[]{:S(2)}, u32[]{:S(2)}) async-start(bf16[2,4,64,16,256]{4,3,1,0,2:T(8,128)(2,1)} %copy.32), calls=%async_computation | async-start | bytes 8388608 | tf_op jit(solution)/shard_map/all_to_all | solution.py:52
  22.8 0.0 copy-done.2
  22.8 0.6 dynamic_slice.28
  24.7 0.6 dynamic_slice.25
  26.5 0.7 dynamic-slice_bitcast_fusion
  27.2 0.0 copy-done.3
  27.2 0.2 convolution_bitcast_fusion
  27.4 0.1 fusion.13
  27.6 0.0 copy-done.4
  27.6 90.4 %all-to-all-done = bf16[2,4,64,16,256]{4,3,1,0,2:T(8,128)(2,1)} async-done(((bf16[2,4,64,16,256]{4,3,1,0,2:T(8,128)(2,1)}), bf16[2,4,64,16,256]{4,3,1,0,2:T(8,128)(2,1)}, u32[]{:S(2)}, u32[]{:S(2)}) %all-to-all-start) | async-done | bytes 4194336 | tf_op jit(solution)/shard_map/all_to_all | solution.py:52
  118.0 4.3 %broadcast_in_dim.30 = f32[2048,1024]{1,0:T(8,128)} broadcast(f32[]{:T(128)} %constant.77.clone.1), dimensions={} | broadcast | bytes 8388612 | tf_op jit(solution)/shard_map/broadcast_in_dim | solution.py:51
  122.3 31.5 %while.10 = (s32[]{:T(128)}, f32[2048,1024]{1,0:T(8,128)}, s32[]{:T(128)}, f32[4]{0:T(128)S(1)}, bf16[2,4,64,16,256]{4,3,1,0,2:T(8,128)(2,1)}, /*index=5*/s32[]{:T(128)}, s32[]{:T(128)}, s32[]{:T(128)}, s32[]{}) while((s32[]{:T(128)}, f32[2048,1024]{1,0:T(8,128)}, s32[]{:T(128)}, f32[4]{0:T(128)S(1)}, bf16[2,4,64,16,256]{4,3,1,0,2:T(8,128)(2,1)}, ...), condition=%wide.region_2.3_spmd, body=%wide.region_1.2_spmd.sunk | while | flops 2162425856 | bytes 21495972 | solution.py:58
  123.0 1.3 constant_dynamic-slice_fusion.4
  124.3 0.1 bitcast_negate_fusion.2
  124.3 0.6 dynamic_slice.42
  124.9 12.8 %multiply_add_fusion.2 = f32[2048,1024]{1,0:T(8,128)} fusion(f32[2048,1024]{1,0:T(8,128)} %get-tuple-element.107, f32[]{:T(128)} %bitcast.53, bf16[1024,256]{1,0:T(8,128)(2,1)S(1)} %bitcast_negate_fusion.2, bf16[1024,256]{1,0:T(8,128)(2,1)S(1)} %bitcast.62, bf16[1024,256]{1,0:T(8,128)(2,1)S(1)} %bitcast.56), kind=kOutput, calls=%fused_computation.2.clone.1 | convolution fusion | flops 2162163712 | bytes 18350084 | tf_op jit(solution)/shard_map/while/body/dot_general | solution.py:17
  138.4 1.3 constant_dynamic-slice_fusion.4
  139.7 0.1 bitcast_negate_fusion.2
  139.8 0.6 dynamic_slice.42
  140.4 12.8 %multiply_add_fusion.2 = f32[2048,1024]{1,0:T(8,128)} fusion(f32[2048,1024]{1,0:T(8,128)} %get-tuple-element.107, f32[]{:T(128)} %bitcast.53, bf16[1024,256]{1,0:T(8,128)(2,1)S(1)} %bitcast_negate_fusion.2, bf16[1024,256]{1,0:T(8,128)(2,1)S(1)} %bitcast.62, bf16[1024,256]{1,0:T(8,128)(2,1)S(1)} %bitcast.56), kind=kOutput, calls=%fused_computation.2.clone.1 | convolution fusion | flops 2162163712 | bytes 18350084 | tf_op jit(solution)/shard_map/while/body/dot_general | solution.py:17
  153.8 4.5 %convert_bitcast_fusion = bf16[256,8,8,128]{3,1,2,0:T(8,128)(2,1)S(1)} fusion(f32[2048,1024]{1,0:T(8,128)} %get-tuple-element.33), kind=kLoop, calls=%fused_computation.19 | loop fusion | flops 2097152 | bytes 12582912
  158.3 1.1 copy.42
  159.4 3.2 copy.34
  162.6 5.2 %gather_fusion.1 = bf16[64,2,128,128]{3,2,1,0:T(8,128)(2,1)} fusion(bf16[64,2,128,128]{3,2,1,0:T(8,128)(2,1)} %bitcast.58, s32[1024]{0:T(1024)S(1)} %pad_clamp_fusion), kind=kCustom, calls=%fused_computation.1 | custom fusion | bytes 8388864 | tf_op jit(solution)/shard_map/jit(_take)/gather | solution.py:63
  167.8 2.6 fusion.11
  170.4 131.7 %all_to_all.28 = bf16[1,64,1,2,128,128]{5,4,3,2,0,1:T(8,128)(2,1)S(1)} all-to-all(bf16[1,64,1,2,128,128]{5,4,3,2,0,1:T(8,128)(2,1)S(1)} %fusion.11), channel_id=1, replica_groups=mesh['stn'=64,'band'=4] {'stn'}, dimensions={1} | all-to-all | bytes 8388608 | tf_op jit(solution)/shard_map/all_to_all | solution.py:65
  302.1 6.3 %copy.36 = bf16[1,64,1,2,128,128]{5,3,1,2,0,4:T(2,128)(2,1)} copy(bf16[1,64,1,2,128,128]{5,4,3,2,0,1:T(8,128)(2,1)S(1)} %all_to_all.28) | data formatting | bytes 8388608 | tf_op jit(solution)/shard_map/all_to_all | solution.py:65
  308.5 53.7 %all_to_all.29 = bf16[1,64,1,2,128,128]{5,3,1,2,0,4:T(2,128)(2,1)S(1)} all-to-all(bf16[1,64,1,2,128,128]{5,3,1,2,0,4:T(2,128)(2,1)} %copy.36), channel_id=1, replica_groups=mesh['stn'=64,'band'=4] {'band'}, dimensions={4} | all-to-all | bytes 8388608 | tf_op jit(solution)/shard_map/all_to_all | solution.py:64
  362.2 4.9 %copy.37 = bf16[1,64,1,2,128,128]{5,4,3,1,2,0:T(8,128)(2,1)S(1)} copy(bf16[1,64,1,2,128,128]{5,3,1,2,0,4:T(2,128)(2,1)S(1)} %all_to_all.29) | data formatting | bytes 8388608 | tf_op jit(solution)/shard_map/all_to_all | solution.py:64
  367.0 0.0 copy-start.1
  367.0 3.2 copy.38
  370.3 0.0 copy-done.1
  (8 shorter events, 0.1 us)
Async XLA Ops:
  0.0 2.0 copy-start
  10.7 12.1 %copy-start.2 = (s32[4,64]{1,0:T(4,128)S(1)}, s32[4,64]{1,0:T(4,128)}, u32[]{:S(2)}) copy-start(s32[4,64]{1,0:T(4,128)} %param.8) | copy-start | bytes 3076
  10.7 16.5 %copy-start.3 = (f32[64]{0:T(128)S(1)}, f32[64]{0:T(128)}, u32[]{:S(2)}) copy-start(f32[64]{0:T(128)} %param.10) | copy-start | bytes 772
  10.7 16.9 %copy-start.4 = (s32[64]{0:T(128)S(1)}, s32[64]{0:T(128)}, u32[]{:S(2)}) copy-start(s32[64]{0:T(128)} %param.11) | copy-start | bytes 772
  10.7 107.3 %all-to-all-start = ((bf16[2,4,64,16,256]{4,3,1,0,2:T(8,128)(2,1)}), bf16[2,4,64,16,256]{4,3,1,0,2:T(8,128)(2,1)}, u32[]{:S(2)}, u32[]{:S(2)}) async-start(bf16[2,4,64,16,256]{4,3,1,0,2:T(8,128)(2,1)} %copy.32), calls=%async_computation | async-start | bytes 8388608 | tf_op jit(solution)/shard_map/all_to_all | solution.py:52
  367.0 3.2 copy-start.1
where the time goes:
time: 371 us; the launch traced here: 370 us
  blocking collectives  185 us (50%)
  waiting for transfers between devices  90.4 us (24%)
  local copies, waits for them, and re-layouts  42.9 us (12%)
  matrix products  25.8 us (7%)
  starting transfers between devices  12.1 us (3%)
  other arithmetic  9.05 us (2%)
    all_to_all x1, blocking collectives, body(): lax.all_to_all(sending, 'stn', split_axis=1, concat_axis=1, tiled=True)  132 us
    all_to_all x1, waiting for transfers between devices, body(): lax.all_to_all(outgoing, 'stn', split_axis=2, concat_axis=2, tiled=True)  90.4 us
    all_to_all x1, blocking collectives, body(): lax.all_to_all(lax.all_to_all(sending, 'stn', split_axis=1, concat_axis=1...  53.7 us
    dot_general x2, matrix products, correlate_full(): lax.dot_general(stacked, right_side, (((1,), (1,)), ((), ())), preferred_...  25.6 us
    all_to_all x1, starting transfers between devices, body(): lax.all_to_all(outgoing, 'stn', split_axis=2, concat_axis=2, tiled=True)  12.1 us
    all_to_all x2, local copies, waits for them, and re-layouts, body(): lax.all_to_all(lax.all_to_all(sending, 'stn', split_axis=1, concat_axis=1...  8.09 us
  transfers between devices with their start and end apart: 1, of which 1 were waited for; matrix products, arithmetic and copies ran while one was open for 1% of the time, Pallas kernels for 0%

commit v1 on v0

v1 whole, which is shorter than its diff:
```python
import functools

import jax
import jax.numpy as jnp
from jax import lax
from jax.experimental import pallas as pl
from jax.experimental.pallas import tpu as pltpu
from jax.sharding import PartitionSpec as P

SP = 1024
TIME = 256
BB = 128
MOST = 4
GROUPS = 64
BANDS = 4
HALF = GROUPS // 2
CHIPS = 32
SLOTS = MOST + 1
SIDE = SP // BB
SUPER = 256
ROWS = BB // BANDS

SMEM = pl.BlockSpec(memory_space=pltpu.SMEM)
VMEM = pl.BlockSpec(memory_space=pltpu.VMEM)


def first_places(count_ref, band):
    def tally(g, held):
        size = count_ref[band, g]
        return tuple(n + (size == s).astype(jnp.int32) for n, s in zip(held, (4, 3, 2)))

    zero = jnp.int32(0)
    fours, threes, twos = lax.fori_loop(0, GROUPS, tally, (zero, zero, zero), unroll=8)
    return zero, fours, fours + threes, fours + threes + twos


def next_place(places, size):
    at = [size == s for s in (4, 3, 2, 1)]
    place = jnp.where(at[0], places[0], jnp.where(at[1], places[1], jnp.where(at[2], places[2], places[3])))
    return place, tuple(p + a.astype(jnp.int32) for p, a in zip(places, at))


def build_kernel(count_ref, volt_ref, send_ref):
    band = lax.axis_index("band")

    def one_group(g, held):
        places, start = held
        size = count_ref[band, g]
        place, places = next_place(places, size)
        large = place < HALF
        chip = jnp.where(large, place, GROUPS - 1 - place)
        base = jnp.where(large, SLOTS - size, 0)

        def one_channel(i, carry):
            for part in range(2):
                send_ref[2 * chip + part, base + i] = volt_ref[part, start + i]
            return carry

        lax.fori_loop(0, size, one_channel, 0)
        return places, start + size

    lax.fori_loop(0, GROUPS, one_group, (first_places(count_ref, band), jnp.int32(0)))


def index_kernel(count_ref, level_ref, gain_ref, order_ref, meta_ref, weight_ref, slot_ref, place_ref):
    mine = lax.axis_index("stn")
    my_band = lax.axis_index("band")
    chip = mine // 2
    meta_ref[4] = lax.rem(mine, 2)

    def one_band(band, carry):
        def one_group(g, held):
            places, start = held
            size = count_ref[band, g]
            place, places = next_place(places, size)
            place_ref[band, g] = place
            own = (band == my_band) & ((place == chip) | (place == GROUPS - 1 - chip))

            @pl.when(own)
            def _():
                large = (place < HALF).astype(jnp.int32)
                meta_ref[large] = size
                base = jnp.where(large == 1, SLOTS - size, 0)
                scale = jnp.where(
                    size == 4,
                    1.0 / (4 * TIME),
                    jnp.where(size == 3, 1.0 / (3 * TIME), jnp.where(size == 2, 1.0 / (2 * TIME), 1.0 / TIME)),
                )

                def one_channel(i, carry):
                    weight_ref[base + i] = gain_ref[level_ref[band, start + i]] * scale
                    return carry

                lax.fori_loop(0, size, one_channel, 0)

            return places, start + size

        lax.fori_loop(0, GROUPS, one_group, (first_places(count_ref, band), jnp.int32(0)))
        return carry

    lax.fori_loop(0, BANDS, one_band, 0)

    def one_slot(s, carry):
        slot_ref[order_ref[s]] = s
        return carry

    lax.fori_loop(0, GROUPS, one_slot, 0, unroll=8)


def visibility_kernel(meta_ref, weight_ref, slot_ref, mine_ref, other_ref, out_ref, left, right, total):
    core = meta_ref[4]
    sign = (1 - 2 * core).astype(jnp.float32)

    for large in range(2):
        size = meta_ref[large]
        base = SLOTS - size if large else 0

        def one_channel(i, carry):
            t = base + i
            weight = weight_ref[t]
            u = mine_ref[:, t].reshape(SP, TIME)
            v = other_ref[:, t].reshape(SP, TIME)
            left[:, :TIME] = u

            @pl.when(core == 0)
            def _():
                left[:, TIME:] = v
                right[:, :TIME] = u
                right[:, TIME:] = v

            @pl.when(core == 1)
            def _():
                left[:, TIME:] = -v
                right[:, :TIME] = v
                right[:, TIME:] = u

            def products(first):
                for row in range(0, SP, SUPER):
                    part = weight * lax.dot_general(
                        left[row : row + SUPER],
                        right[row:],
                        (((1,), (1,)), ((), ())),
                        preferred_element_type=jnp.float32,
                    )
                    if first:
                        total[row : row + SUPER, row:] = part
                    else:
                        total[row : row + SUPER, row:] += part

            @pl.when(i == 0)
            def _():
                products(True)

            @pl.when(i > 0)
            def _():
                products(False)

            return carry

        lax.fori_loop(0, size, one_channel, 0)

        def store(p, q, block):
            out_ref[slot_ref[SIDE * p + q], :, large] = block.astype(jnp.bfloat16).reshape(BANDS, ROWS, BB)

        per = SUPER // BB
        for p in range(SIDE):
            for q in range(p // per * per, SIDE):
                block = total[p * BB : (p + 1) * BB, q * BB : (q + 1) * BB]
                store(p, q, block)
                if q // per > p // per:
                    store(q, p, sign * block.T)


def place_kernel(place_ref, got_ref, out_ref):
    step = pl.program_id(0)
    per = out_ref.shape[0]

    def one_group(i, carry):
        for band in range(BANDS):
            place = place_ref[band, step * per + i]
            large = (place < HALF).astype(jnp.int32)
            chip = jnp.where(place < HALF, place, GROUPS - 1 - place)
            out_ref[i, band] = got_ref[chip, :, band, large]
        return carry

    lax.fori_loop(0, per, one_group, 0)


def body(voltages, group_count, levels, bandpass, block_order):
    stations, samples = voltages.shape[2], voltages.shape[3]
    owners = lax.axis_size("stn")
    sending = pl.pallas_call(
        build_kernel,
        out_shape=jax.ShapeDtypeStruct((owners, SLOTS, stations, samples), jnp.bfloat16),
        in_specs=[SMEM, VMEM],
        out_specs=VMEM,
        cost_estimate=pl.CostEstimate(flops=0, bytes_accessed=5 << 20, transcendentals=0),
        name="build",
    )(group_count, voltages)
    meta, weights, slots, places = pl.pallas_call(
        index_kernel,
        out_shape=(
            jax.ShapeDtypeStruct((8,), jnp.int32),
            jax.ShapeDtypeStruct((8,), jnp.float32),
            jax.ShapeDtypeStruct((GROUPS,), jnp.int32),
            jax.ShapeDtypeStruct((BANDS, GROUPS), jnp.int32),
        ),
        in_specs=[SMEM] * 4,
        out_specs=(SMEM,) * 4,
        cost_estimate=pl.CostEstimate(flops=0, bytes_accessed=8 << 20, transcendentals=0),
        name="index",
    )(group_count, levels, bandpass, block_order)
    mine = lax.all_to_all(sending, "stn", split_axis=0, concat_axis=0, tiled=True)
    other = lax.ppermute(mine, "stn", [(i, i ^ 1) for i in range(owners)])
    blocks = pl.pallas_call(
        visibility_kernel,
        out_shape=jax.ShapeDtypeStruct((GROUPS, BANDS, 2, ROWS, BB), jnp.bfloat16),
        in_specs=[SMEM, SMEM, SMEM, VMEM, VMEM],
        out_specs=VMEM,
        scratch_shapes=[
            pltpu.VMEM((SP, 2 * TIME), jnp.bfloat16),
            pltpu.VMEM((SP, 2 * TIME), jnp.bfloat16),
            pltpu.VMEM((SP, SP), jnp.float32),
        ],
        cost_estimate=pl.CostEstimate(flops=4 << 30, bytes_accessed=9 << 20, transcendentals=0),
        name="visibility",
    )(meta, weights, slots, mine, other)
    blocks = blocks.reshape(GROUPS * BANDS, 2, ROWS, BB)
    got = lax.all_to_all(blocks, ("stn", "band"), split_axis=0, concat_axis=0, tiled=True)
    got = got.reshape(CHIPS, 2, BANDS, 2, ROWS, BB)
    steps = 8
    out = pl.pallas_call(
        place_kernel,
        grid=(steps,),
        out_shape=jax.ShapeDtypeStruct((GROUPS, BANDS, 2, ROWS, BB), jnp.bfloat16),
        in_specs=[SMEM, VMEM],
        out_specs=pl.BlockSpec((GROUPS // steps, BANDS, 2, ROWS, BB), lambda i: (i, 0, 0, 0, 0)),
        cost_estimate=pl.CostEstimate(flops=0, bytes_accessed=8 << 20, transcendentals=0),
        name="place",
    )(places, got)
    return out.reshape(1, GROUPS, BANDS, 2, ROWS, BB)


def solution(mesh):
    return jax.shard_map(
        body,
        mesh=mesh,
        in_specs=(P(None, "band", "stn", None), P(), P(), P(), P()),
        out_specs=P("stn", None, None, None, "band", None),
        check_vma=False,
    )
```

time: 371 us -> 214 us (0.58)
  waiting for transfers between devices: 90.4 us -> 0.01 us
  local copies, waits for them, and re-layouts: 42.9 us -> 0.01 us
  Pallas kernels: 0 us -> 31.5 us
  matrix products: 25.8 us -> 0 us
  starting transfers between devices: 12.1 us -> 0.47 us
  other arithmetic: 9.05 us -> 0 us
  blocking collectives: 185 us -> 179 us
    all_to_all x1 -> x0, waiting for transfers between devices: 90.4 us -> none  [body(): lax.all_to_all(outgoing, 'stn', split_axis=2, concat_axis=2, tiled=True)]
    pallas_call x0 -> x4, Pallas kernels: none -> 31.5 us  [the longest x1 11 us: body(): pl.pallas_call(visibility_kernel, out_shape=jax.ShapeDtypeStruct((GROUPS,...]
    dot_general x3 -> x0, matrix products: 25.8 us -> none  [the longest x2 25.6 us: correlate_full(): lax.dot_general(stacked, right_side, (((1,), (1,)), ((), ())), preferred_...]
    all_to_all x3 -> x0, local copies, waits for them, and re-layouts: 14.4 us -> none  [the longest x2 8.09 us: body(): lax.all_to_all(lax.all_to_all(sending, 'stn', split_axis=1, concat_axis=1...]
    all_to_all x1 -> x0, starting transfers between devices: 12.1 us -> none  [body(): lax.all_to_all(outgoing, 'stn', split_axis=2, concat_axis=2, tiled=True)]
    gather x3 -> x0, local copies, waits for them, and re-layouts: 10.6 us -> none  [the longest x2 5.35 us: body(): jnp.take(voltages, picked, axis=1)]
    all_to_all x2, blocking collectives: 185 us -> 179 us  [the longest x1 106 us: body(): lax.all_to_all(blocks, ('stn', 'band'), split_axis=0, concat_axis=0, tile...]
    unnamed x1 -> x0, other arithmetic: 4.48 us -> none
  transfers between devices with their start and end apart: 1 -> 1, of which waited for: 1 -> 0; matrix products, arithmetic and copies ran while one was open for 1% -> 0% of each run, Pallas kernels for 0% -> 4%
where the time goes in v1:
time: 214 us; the launch traced here: 211 us
  blocking collectives  179 us (84%)
  Pallas kernels  31.5 us (15%)
    all_to_all x1, blocking collectives, body(): lax.all_to_all(blocks, ('stn', 'band'), split_axis=0, concat_axis=0, tile...  106 us
    all_to_all x1, blocking collectives, body(): lax.all_to_all(sending, 'stn', split_axis=0, concat_axis=0, tiled=True)  73.4 us
    pallas_call x1, Pallas kernels, body(): pl.pallas_call(visibility_kernel, out_shape=jax.ShapeDtypeStruct((GROUPS,...  11 us
    pallas_call x1, Pallas kernels, body(): pl.pallas_call(index_kernel, out_shape=(jax.ShapeDtypeStruct((8,), jnp.in...  8.87 us
    pallas_call x1, Pallas kernels, body(): pl.pallas_call(place_kernel, grid=(steps,), out_shape=jax.ShapeDtypeStruc...  6.19 us
    pallas_call x1, Pallas kernels, body(): pl.pallas_call(build_kernel, out_shape=jax.ShapeDtypeStruct((owners, SLOT...  5.4 us
  transfers between devices with their start and end apart: 1, of which 0 were waited for; matrix products, arithmetic and copies ran while one was open for 0% of the time, Pallas kernels for 4%

profile of v1, /device:TPU:32, one launch (start us, length us, event | category | flops | bytes accessed | tf_op | source)
XLA Modules:
  0.0 211.0 jit_solution(2644914293410951844)
XLA Ops:
  0.0 5.4 %build.1 = bf16[64,5,16,256]{3,2,1,0:T(8,128)(2,1)} custom-call(s32[4,64]{1,0:T(4,128)} %count_ref.3, bf16[2,128,16,256]{3,2,1,0:T(8,128)(2,1)} %volt_ref.1), custom_call_target="tpu_custom_call" | custom-call | bytes 5242880 | tf_op jit(solution)/shard_map/build/pallas_call | solution.py:192
  5.4 73.4 %all_to_all.10.mine_ref = bf16[64,5,16,256]{3,2,1,0:T(8,128)(2,1)S(1)} all-to-all(bf16[64,5,16,256]{3,2,1,0:T(8,128)(2,1)} %build.1), channel_id=1, replica_groups=mesh['stn'=64,'band'=4] {'stn'}, dimensions={0} | all-to-all | bytes 5242880 | tf_op jit(solution)/shard_map/all_to_all | solution.py:213
  78.8 0.0 copy-start
  78.8 0.5 collective-permute-start
  79.2 8.9 %index.1 = (s32[8]{0:T(128)}, f32[8]{0:T(128)}, s32[64]{0:T(128)}, s32[4,64]{1,0:T(4,128)}) custom-call(s32[4,64]{1,0:T(4,128)} %count_ref.3, s32[4,128]{1,0:T(4,128)} %level_ref.1, f32[64]{0:T(128)} %gain_ref.1, s32[64]{0:T(128)} %order_ref.1), custom_call_target="tpu_custom_call" | custom-call | bytes 8388608 | tf_op jit(solution)/shard_map/index/pallas_call | solution.py:200
  88.1 0.0 collective-permute-done.other_ref
  88.1 0.0 copy-done
  88.1 11.0 %visibility.1 = bf16[64,4,2,32,128]{4,3,2,1,0:T(8,128)(2,1)} custom-call(s32[8]{0:T(128)} %get-tuple-element.10.meta_ref, f32[8]{0:T(128)} %get-tuple-element.11.weight_ref, s32[64]{0:T(128)} %get-tuple-element.12.slot_ref, bf16[64,5,16,256]{3,2,1,0:T(8,128)(2,1)} %copy-done, bf16[64,5,16,256]{3,2,1,0:T(8,128)(2,1)} %collective-permute-done.other_ref), custom_call_target="tpu_custom_call" | custom-call | flops 4294967296 | bytes 9437184 | tf_op jit(solution)/shard_map/visibility/pallas_call | solution.py:215
  99.2 105.6 %all_to_all.11 = bf16[256,2,32,128]{3,2,1,0:T(8,128)(2,1)} all-to-all(bf16[256,2,32,128]{3,2,1,0:T(8,128)(2,1)} %bitcast.4), channel_id=1, replica_groups=mesh['stn'=64,'band'=4] {'stn','band'}, dimensions={0} | all-to-all | bytes 8388608 | tf_op jit(solution)/shard_map/all_to_all | solution.py:229
  204.8 6.2 %place.1 = bf16[64,4,2,32,128]{4,3,2,1,0:T(8,128)(2,1)} custom-call(s32[4,64]{1,0:T(4,128)} %get-tuple-element.9.place_ref, bf16[32,2,4,2,32,128]{5,4,3,2,1,0:T(8,128)(2,1)} %bitcast.3), custom_call_target="tpu_custom_call" | custom-call | bytes 8388608 | tf_op jit(solution)/shard_map/place/pallas_call | solution.py:232
Async XLA Ops:
  78.8 9.4 %copy-start = (bf16[64,5,16,256]{3,2,1,0:T(8,128)(2,1)}, bf16[64,5,16,256]{3,2,1,0:T(8,128)(2,1)S(1)}, u32[]{:S(2)}) copy-start(bf16[64,5,16,256]{3,2,1,0:T(8,128)(2,1)S(1)} %all_to_all.10.mine_ref) | copy-start | bytes 7864324
  78.8 9.4 %collective-permute-start = (bf16[64,5,16,256]{3,2,1,0:T(8,128)(2,1)S(1)}, bf16[64,5,16,256]{3,2,1,0:T(8,128)(2,1)}, u32[]{:S(2)}, u32[]{:S(2)}) collective-permute-start(bf16[64,5,16,256]{3,2,1,0:T(8,128)(2,1)S(1)} %all_to_all.10.mine_ref), channel_id=1, source_target_pairs={{0,4},{4,0},{8,12},{12,8},{16,20},{20,16},{24,28},{28,24},{32,36},... | collective-permute-start | bytes 7864328 | tf_op jit(solution)/shard_map/ppermute | solution.py:214

commit v2 on v1

--- a/solution.py
+++ b/solution.py
@@ -1,11 +1,10 @@
-import functools
-
 import jax
 import jax.numpy as jnp
 from jax import lax
 from jax.experimental import pallas as pl
 from jax.experimental.pallas import tpu as pltpu
 from jax.sharding import PartitionSpec as P
+
 
 SP = 1024
 TIME = 256
@@ -22,6 +21,7 @@
 
 SMEM = pl.BlockSpec(memory_space=pltpu.SMEM)
 VMEM = pl.BlockSpec(memory_space=pltpu.VMEM)
+ANY = pl.BlockSpec(memory_space=pl.ANY)
 
 
 def first_places(count_ref, band):
@@ -40,26 +40,27 @@
     return place, tuple(p + a.astype(jnp.int32) for p, a in zip(places, at))
 
 
-def build_kernel(count_ref, volt_ref, send_ref):
+def build_kernel(count_ref, volt_ref, send_ref, held, arrival):
     band = lax.axis_index("band")
-
-    def one_group(g, held):
-        places, start = held
+    copy = pltpu.make_async_copy(volt_ref, held, arrival)
+    copy.start()
+    places = first_places(count_ref, band)
+    copy.wait()
+
+    def one_group(g, carry):
+        places, start = carry
         size = count_ref[band, g]
         place, places = next_place(places, size)
         large = place < HALF
         chip = jnp.where(large, place, GROUPS - 1 - place)
         base = jnp.where(large, SLOTS - size, 0)
-
-        def one_channel(i, carry):
+        for i in range(MOST):
+            step = jnp.minimum(i, size - 1)
             for part in range(2):
-                send_ref[2 * chip + part, base + i] = volt_ref[part, start + i]
-            return carry
-
-        lax.fori_loop(0, size, one_channel, 0)
+                send_ref[2 * chip + part, base + step] = held[part, start + step]
         return places, start + size
 
-    lax.fori_loop(0, GROUPS, one_group, (first_places(count_ref, band), jnp.int32(0)))
+    lax.fori_loop(0, GROUPS, one_group, (places, jnp.int32(0)), unroll=4)
 
 
 def index_kernel(count_ref, level_ref, gain_ref, order_ref, meta_ref, weight_ref, slot_ref, place_ref):
@@ -107,9 +108,11 @@
     lax.fori_loop(0, GROUPS, one_slot, 0, unroll=8)
 
 
-def visibility_kernel(meta_ref, weight_ref, slot_ref, mine_ref, other_ref, out_ref, left, right, total):
+def visibility_kernel(meta_ref, weight_ref, slot_ref, mine_ref, other_ref, out_ref, total):
     core = meta_ref[4]
     sign = (1 - 2 * core).astype(jnp.float32)
+    stations = mine_ref.shape[2]
+    tall = SUPER // stations
 
     for large in range(2):
         size = meta_ref[large]
@@ -118,27 +121,21 @@
         def one_channel(i, carry):
             t = base + i
             weight = weight_ref[t]
-            u = mine_ref[:, t].reshape(SP, TIME)
-            v = other_ref[:, t].reshape(SP, TIME)
-            left[:, :TIME] = u
-
-            @pl.when(core == 0)
-            def _():
-                left[:, TIME:] = v
-                right[:, :TIME] = u
-                right[:, TIME:] = v
-
-            @pl.when(core == 1)
-            def _():
-                left[:, TIME:] = -v
-                right[:, :TIME] = v
-                right[:, TIME:] = u
-
-            def products(first):
+
+            def products(first, imaginary):
                 for row in range(0, SP, SUPER):
+                    r = row // stations
+                    u = mine_ref[r : r + tall, t].reshape(SUPER, TIME)
+                    v = other_ref[r : r + tall, t].reshape(SUPER, TIME)
+                    all_u = mine_ref[r:, t].reshape(SP - row, TIME)
+                    all_v = other_ref[r:, t].reshape(SP - row, TIME)
+                    if imaginary:
+                        left, right = (u, -v), (all_v, all_u)
+                    else:
+                        left, right = (u, v), (all_u, all_v)
                     part = weight * lax.dot_general(
-                        left[row : row + SUPER],
-                        right[row:],
+                        jnp.concatenate(left, 1),
+                        jnp.concatenate(right, 1),
                         (((1,), (1,)), ((), ())),
                         preferred_element_type=jnp.float32,
                     )
@@ -147,13 +144,15 @@
                     else:
                         total[row : row + SUPER, row:] += part
 
-            @pl.when(i == 0)
-            def _():
-                products(True)
-
-            @pl.when(i > 0)
-            def _():
-                products(False)
+            for imaginary in range(2):
+
+                @pl.when((core == imaginary) & (i == 0))
+                def _():
+                    products(True, imaginary)
+
+                @pl.when((core == imaginary) & (i > 0))
+                def _():
+                    products(False, imaginary)
 
             return carry
 
@@ -171,19 +170,18 @@
                     store(q, p, sign * block.T)
 
 
-def place_kernel(place_ref, got_ref, out_ref):
-    step = pl.program_id(0)
-    per = out_ref.shape[0]
-
-    def one_group(i, carry):
-        for band in range(BANDS):
-            place = place_ref[band, step * per + i]
+def place_kernel(place_ref, got_ref, out_ref, landed):
+    for band in range(BANDS):
+
+        def one_group(g, carry):
+            place = place_ref[band, g]
             large = (place < HALF).astype(jnp.int32)
             chip = jnp.where(place < HALF, place, GROUPS - 1 - place)
-            out_ref[i, band] = got_ref[chip, :, band, large]
-        return carry
-
-    lax.fori_loop(0, per, one_group, 0)
+            pltpu.make_async_copy(got_ref.at[chip, :, band, large], out_ref.at[g, band], landed).start()
+            return carry
+
+        lax.fori_loop(0, GROUPS, one_group, 0, unroll=8)
+    pltpu.make_async_copy(out_ref, out_ref, landed).wait()
 
 
 def body(voltages, group_count, levels, bandpass, block_order):
@@ -192,8 +190,9 @@
     sending = pl.pallas_call(
         build_kernel,
         out_shape=jax.ShapeDtypeStruct((owners, SLOTS, stations, samples), jnp.bfloat16),
-        in_specs=[SMEM, VMEM],
+        in_specs=[SMEM, ANY],
         out_specs=VMEM,
+        scratch_shapes=[pltpu.VMEM(voltages.shape, voltages.dtype), pltpu.SemaphoreType.DMA],
         cost_estimate=pl.CostEstimate(flops=0, bytes_accessed=5 << 20, transcendentals=0),
         name="build",
     )(group_count, voltages)
@@ -208,6 +207,7 @@
         in_specs=[SMEM] * 4,
         out_specs=(SMEM,) * 4,
         cost_estimate=pl.CostEstimate(flops=0, bytes_accessed=8 << 20, transcendentals=0),
+        compiler_params=pltpu.CompilerParams(vmem_limit_bytes=2 << 20),
         name="index",
     )(group_count, levels, bandpass, block_order)
     mine = lax.all_to_all(sending, "stn", split_axis=0, concat_axis=0, tiled=True)
@@ -218,24 +218,23 @@
         in_specs=[SMEM, SMEM, SMEM, VMEM, VMEM],
         out_specs=VMEM,
         scratch_shapes=[
-            pltpu.VMEM((SP, 2 * TIME), jnp.bfloat16),
-            pltpu.VMEM((SP, 2 * TIME), jnp.bfloat16),
             pltpu.VMEM((SP, SP), jnp.float32),
         ],
         cost_estimate=pl.CostEstimate(flops=4 << 30, bytes_accessed=9 << 20, transcendentals=0),
+        compiler_params=pltpu.CompilerParams(vmem_limit_bytes=24 << 20),
         name="visibility",
     )(meta, weights, slots, mine, other)
     blocks = blocks.reshape(GROUPS * BANDS, 2, ROWS, BB)
     got = lax.all_to_all(blocks, ("stn", "band"), split_axis=0, concat_axis=0, tiled=True)
     got = got.reshape(CHIPS, 2, BANDS, 2, ROWS, BB)
-    steps = 8
     out = pl.pallas_call(
         place_kernel,
-        grid=(steps,),
         out_shape=jax.ShapeDtypeStruct((GROUPS, BANDS, 2, ROWS, BB), jnp.bfloat16),
         in_specs=[SMEM, VMEM],
-        out_specs=pl.BlockSpec((GROUPS // steps, BANDS, 2, ROWS, BB), lambda i: (i, 0, 0, 0, 0)),
+        out_specs=ANY,
+        scratch_shapes=[pltpu.SemaphoreType.DMA],
         cost_estimate=pl.CostEstimate(flops=0, bytes_accessed=8 << 20, transcendentals=0),
+        compiler_params=pltpu.CompilerParams(vmem_limit_bytes=8 << 20),
         name="place",
     )(places, got)
     return out.reshape(1, GROUPS, BANDS, 2, ROWS, BB)

time: 214 us -> 205 us (0.958)
  Pallas kernels: 31.5 us -> 23.1 us
    pallas_call x1, Pallas kernels: 11 us -> 6.13 us  [body(): pl.pallas_call(visibility_kernel, out_shape=jax.ShapeDtypeStruct((GROUPS,...]
    pallas_call x1, Pallas kernels: 6.19 us -> 2.7 us  [body(): pl.pallas_call(place_kernel, out_shape=jax.ShapeDtypeStruct((GROUPS, BAND...]
where the time goes in v2:
time: 205 us; the launch traced here: 203 us
  blocking collectives  179 us (87%)
  Pallas kernels  23.1 us (11%)
    all_to_all x1, blocking collectives, body(): lax.all_to_all(blocks, ('stn', 'band'), split_axis=0, concat_axis=0, tile...  105 us
    all_to_all x1, blocking collectives, body(): lax.all_to_all(sending, 'stn', split_axis=0, concat_axis=0, tiled=True)  73.5 us
    pallas_call x1, Pallas kernels, body(): pl.pallas_call(index_kernel, out_shape=(jax.ShapeDtypeStruct((8,), jnp.in...  8.78 us
    pallas_call x1, Pallas kernels, body(): pl.pallas_call(visibility_kernel, out_shape=jax.ShapeDtypeStruct((GROUPS,...  6.13 us
    pallas_call x1, Pallas kernels, body(): pl.pallas_call(build_kernel, out_shape=jax.ShapeDtypeStruct((owners, SLOT...  5.49 us
  transfers between devices with their start and end apart: 1, of which 0 were waited for; matrix products, arithmetic and copies ran while one was open for 0% of the time, Pallas kernels for 4%

profile of v2, /device:TPU:32, one launch (start us, length us, event | category | flops | bytes accessed | tf_op | source)
XLA Modules:
  0.0 202.5 jit_solution(15095537491463178228)
XLA Ops:
  0.0 5.5 %build.1 = bf16[64,5,16,256]{3,2,1,0:T(8,128)(2,1)} custom-call(s32[4,64]{1,0:T(4,128)} %count_ref.3, bf16[2,128,16,256]{3,2,1,0:T(8,128)(2,1)} %volt_ref.1), custom_call_target="tpu_custom_call" | custom-call | bytes 5242880 | tf_op jit(solution)/shard_map/build/pallas_call | solution.py:190
  5.5 0.0 copy-start
  5.5 0.0 copy-start.1
  5.5 0.0 copy-start.2
  5.5 0.0 copy-start.3
  5.5 73.5 %all_to_all.10.mine_ref = bf16[64,5,16,256]{3,2,1,0:T(8,128)(2,1)S(1)} all-to-all(bf16[64,5,16,256]{3,2,1,0:T(8,128)(2,1)} %build.1), channel_id=1, replica_groups=mesh['stn'=64,'band'=4] {'stn'}, dimensions={0} | all-to-all | bytes 5242880 | tf_op jit(solution)/shard_map/all_to_all | solution.py:213
  79.1 0.5 collective-permute-start
  79.5 0.0 copy-done
  79.5 0.0 copy-done.1
  79.5 0.0 copy-done.2
  79.5 0.0 copy-done.3
  79.6 8.8 %index.1 = (s32[8]{0:T(128)S(1)}, f32[8]{0:T(128)S(1)}, s32[64]{0:T(128)S(1)}, s32[4,64]{1,0:T(4,128)S(1)}) custom-call(s32[4,64]{1,0:T(4,128)S(1)} %copy-done, s32[4,128]{1,0:T(4,128)S(1)} %copy-done.1, f32[64]{0:T(128)S(1)} %copy-done.2, s32[64]{0:T(128)S(1)} %copy-done.3), custom_call_target="tpu_custom_call" | custom-call | bytes 8388608 | tf_op jit(solution)/shard_map/index/pallas_call | solution.py:199
  88.3 0.0 collective-permute-done.other_ref
  88.4 6.1 %visibility.1 = bf16[64,4,2,32,128]{4,3,2,1,0:T(8,128)(2,1)S(1)} custom-call(s32[8]{0:T(128)S(1)} %get-tuple-element.10.meta_ref, f32[8]{0:T(128)S(1)} %get-tuple-element.11.weight_ref, s32[64]{0:T(128)S(1)} %get-tuple-element.12.slot_ref, bf16[64,5,16,256]{3,2,1,0:T(8,128)(2,1)S(1)} %all_to_all.10.mine_ref, ...), custom_call_target="tpu_custom_call" | custom-call | flops 4294967296 | bytes 9437184 | tf_op jit(solution)/shard_map/visibility/pallas_call | solution.py:215
  94.5 105.3 %all_to_all.11 = bf16[256,2,32,128]{3,2,1,0:T(8,128)(2,1)S(1)} all-to-all(bf16[256,2,32,128]{3,2,1,0:T(8,128)(2,1)S(1)} %bitcast.4), channel_id=1, replica_groups=mesh['stn'=64,'band'=4] {'stn','band'}, dimensions={0} | all-to-all | bytes 8388608 | tf_op jit(solution)/shard_map/all_to_all | solution.py:228
  199.8 2.7 %place.1 = bf16[64,4,2,32,128]{4,3,2,1,0:T(8,128)(2,1)} custom-call(s32[4,64]{1,0:T(4,128)S(1)} %get-tuple-element.9.place_ref, bf16[32,2,4,2,32,128]{5,4,3,2,1,0:T(8,128)(2,1)S(1)} %bitcast.3), custom_call_target="tpu_custom_call" | custom-call | bytes 8388608 | tf_op jit(solution)/shard_map/place/pallas_call | solution.py:230
Async XLA Ops:
  5.5 74.0 %copy-start = (s32[4,64]{1,0:T(4,128)S(1)}, s32[4,64]{1,0:T(4,128)}, u32[]{:S(2)}) copy-start(s32[4,64]{1,0:T(4,128)} %count_ref.3) | copy-start | bytes 3076
  5.5 74.0 %copy-start.1 = (s32[4,128]{1,0:T(4,128)S(1)}, s32[4,128]{1,0:T(4,128)}, u32[]{:S(2)}) copy-start(s32[4,128]{1,0:T(4,128)} %level_ref.1) | copy-start | bytes 6148
  5.5 74.0 %copy-start.2 = (f32[64]{0:T(128)S(1)}, f32[64]{0:T(128)}, u32[]{:S(2)}) copy-start(f32[64]{0:T(128)} %gain_ref.1) | copy-start | bytes 772
  5.5 74.0 %copy-start.3 = (s32[64]{0:T(128)S(1)}, s32[64]{0:T(128)}, u32[]{:S(2)}) copy-start(s32[64]{0:T(128)} %order_ref.1) | copy-start | bytes 772
  79.1 9.3 %collective-permute-start = (bf16[64,5,16,256]{3,2,1,0:T(8,128)(2,1)S(1)}, bf16[64,5,16,256]{3,2,1,0:T(8,128)(2,1)S(1)}, u32[]{:S(2)}, u32[]{:S(2)}) collective-permute-start(bf16[64,5,16,256]{3,2,1,0:T(8,128)(2,1)S(1)} %all_to_all.10.mine_ref), channel_id=1, source_target_pairs={{0,4},{4,0},{8,12},{12,8},{16,20},{20,16},{24,28},{28,24},{32,36},... | collective-permute-start | bytes 7864328 | tf_op jit(solution)/shard_map/ppermute | solution.py:214

commit v3 on v2

--- a/solution.py
+++ b/solution.py
@@ -1,3 +1,5 @@
+import functools
+
 import jax
 import jax.numpy as jnp
 from jax import lax
@@ -27,11 +29,10 @@
 def first_places(count_ref, band):
     def tally(g, held):
         size = count_ref[band, g]
-        return tuple(n + (size == s).astype(jnp.int32) for n, s in zip(held, (4, 3, 2)))
+        return tuple(n + (size >= s).astype(jnp.int32) for n, s in zip(held, (4, 3, 2)))
 
     zero = jnp.int32(0)
-    fours, threes, twos = lax.fori_loop(0, GROUPS, tally, (zero, zero, zero), unroll=8)
-    return zero, fours, fours + threes, fours + threes + twos
+    return zero, *lax.fori_loop(0, GROUPS, tally, (zero, zero, zero), unroll=True)
 
 
 def next_place(places, size):
@@ -40,27 +41,34 @@
     return place, tuple(p + a.astype(jnp.int32) for p, a in zip(places, at))
 
 
-def build_kernel(count_ref, volt_ref, send_ref, held, arrival):
+def build_kernel(count_ref, volt_ref, send_ref, count, held, arrivals, sent):
     band = lax.axis_index("band")
-    copy = pltpu.make_async_copy(volt_ref, held, arrival)
-    copy.start()
-    places = first_places(count_ref, band)
-    copy.wait()
+    count_copy = pltpu.make_async_copy(count_ref, count, arrivals.at[0])
+    volt_copy = pltpu.make_async_copy(volt_ref, held, arrivals.at[1])
+    count_copy.start()
+    volt_copy.start()
+    count_copy.wait()
+    places = first_places(count, band)
+    volt_copy.wait()
 
     def one_group(g, carry):
         places, start = carry
-        size = count_ref[band, g]
+        size = count[band, g]
         place, places = next_place(places, size)
         large = place < HALF
         chip = jnp.where(large, place, GROUPS - 1 - place)
         base = jnp.where(large, SLOTS - size, 0)
-        for i in range(MOST):
-            step = jnp.minimum(i, size - 1)
-            for part in range(2):
-                send_ref[2 * chip + part, base + step] = held[part, start + step]
+
+        def send(i):
+            pltpu.make_async_copy(held.at[:, start + i], send_ref.at[pl.ds(2 * chip, 2), base + i], sent).start()
+
+        send(0)
+        for i in range(1, MOST):
+            pl.when(i < size)(functools.partial(send, i))
         return places, start + size
 
     lax.fori_loop(0, GROUPS, one_group, (places, jnp.int32(0)), unroll=4)
+    pltpu.make_async_copy(held, held, sent).wait()
 
 
 def index_kernel(count_ref, level_ref, gain_ref, order_ref, meta_ref, weight_ref, slot_ref, place_ref):
@@ -159,15 +167,15 @@
         lax.fori_loop(0, size, one_channel, 0)
 
         def store(p, q, block):
-            out_ref[slot_ref[SIDE * p + q], :, large] = block.astype(jnp.bfloat16).reshape(BANDS, ROWS, BB)
+            out_ref[slot_ref[SIDE * p + q], :, large] = block.reshape(BANDS, ROWS, BB)
 
         per = SUPER // BB
         for p in range(SIDE):
             for q in range(p // per * per, SIDE):
                 block = total[p * BB : (p + 1) * BB, q * BB : (q + 1) * BB]
-                store(p, q, block)
+                store(p, q, block.astype(jnp.bfloat16))
                 if q // per > p // per:
-                    store(q, p, sign * block.T)
+                    store(q, p, (sign * block).astype(jnp.bfloat16).T)
 
 
 def place_kernel(place_ref, got_ref, out_ref, landed):
@@ -190,9 +198,14 @@
     sending = pl.pallas_call(
         build_kernel,
         out_shape=jax.ShapeDtypeStruct((owners, SLOTS, stations, samples), jnp.bfloat16),
-        in_specs=[SMEM, ANY],
-        out_specs=VMEM,
-        scratch_shapes=[pltpu.VMEM(voltages.shape, voltages.dtype), pltpu.SemaphoreType.DMA],
+        in_specs=[ANY, ANY],
+        out_specs=ANY,
+        scratch_shapes=[
+            pltpu.SMEM(group_count.shape, group_count.dtype),
+            pltpu.VMEM(voltages.shape, voltages.dtype),
+            pltpu.SemaphoreType.DMA((2,)),
+            pltpu.SemaphoreType.DMA,
+        ],
         cost_estimate=pl.CostEstimate(flops=0, bytes_accessed=5 << 20, transcendentals=0),
         name="build",
     )(group_count, voltages)

time: 205 us -> 202 us (0.985)
  Pallas kernels: 23.1 us -> 19.7 us
    pallas_call x1, Pallas kernels: 5.49 us -> 3.18 us  [body(): pl.pallas_call(build_kernel, out_shape=jax.ShapeDtypeStruct((owners, SLOT...]
where the time goes in v3:
time: 202 us; the launch traced here: 199 us
  blocking collectives  179 us (89%)
  Pallas kernels  19.7 us (10%)
    all_to_all x1, blocking collectives, body(): lax.all_to_all(blocks, ('stn', 'band'), split_axis=0, concat_axis=0, tile...  105 us
    all_to_all x1, blocking collectives, body(): lax.all_to_all(sending, 'stn', split_axis=0, concat_axis=0, tiled=True)  73.5 us
    pallas_call x1, Pallas kernels, body(): pl.pallas_call(index_kernel, out_shape=(jax.ShapeDtypeStruct((8,), jnp.in...  8.04 us
    pallas_call x1, Pallas kernels, body(): pl.pallas_call(visibility_kernel, out_shape=jax.ShapeDtypeStruct((GROUPS,...  5.76 us
  transfers between devices with their start and end apart: 1, of which 0 were waited for; matrix products, arithmetic and copies ran while one was open for 0% of the time, Pallas kernels for 4%

profile of v3, /device:TPU:32, one launch (start us, length us, event | category | flops | bytes accessed | tf_op | source)
XLA Modules:
  0.0 199.1 jit_solution(17421686922991792357)
XLA Ops:
  0.0 3.2 %build.1 = bf16[64,5,16,256]{3,2,1,0:T(8,128)(2,1)} custom-call(s32[4,64]{1,0:T(4,128)} %count_ref.3, bf16[2,128,16,256]{3,2,1,0:T(8,128)(2,1)} %volt_ref.1), custom_call_target="tpu_custom_call" | custom-call | bytes 5242880 | tf_op jit(solution)/shard_map/build/pallas_call | solution.py:198
  3.2 0.0 copy-start
  3.2 0.0 copy-start.1
  3.2 0.0 copy-start.2
  3.2 0.0 copy-start.3
  3.2 73.5 %all_to_all.10.mine_ref = bf16[64,5,16,256]{3,2,1,0:T(8,128)(2,1)S(1)} all-to-all(bf16[64,5,16,256]{3,2,1,0:T(8,128)(2,1)} %build.1), channel_id=1, replica_groups=mesh['stn'=64,'band'=4] {'stn'}, dimensions={0} | all-to-all | bytes 5242880 | tf_op jit(solution)/shard_map/all_to_all | solution.py:226
  76.8 0.5 collective-permute-start
  77.2 0.0 copy-done
  77.2 0.0 copy-done.1
  77.2 0.0 copy-done.2
  77.2 0.0 copy-done.3
  77.2 8.0 %index.1 = (s32[8]{0:T(128)S(1)}, f32[8]{0:T(128)S(1)}, s32[64]{0:T(128)S(1)}, s32[4,64]{1,0:T(4,128)S(1)}) custom-call(s32[4,64]{1,0:T(4,128)S(1)} %copy-done, s32[4,128]{1,0:T(4,128)S(1)} %copy-done.1, f32[64]{0:T(128)S(1)} %copy-done.2, s32[64]{0:T(128)S(1)} %copy-done.3), custom_call_target="tpu_custom_call" | custom-call | bytes 8388608 | tf_op jit(solution)/shard_map/index/pallas_call | solution.py:212
  85.3 0.0 collective-permute-done.other_ref
  85.3 5.8 %visibility.1 = bf16[64,4,2,32,128]{4,3,2,1,0:T(8,128)(2,1)S(1)} custom-call(s32[8]{0:T(128)S(1)} %get-tuple-element.10.meta_ref, f32[8]{0:T(128)S(1)} %get-tuple-element.11.weight_ref, s32[64]{0:T(128)S(1)} %get-tuple-element.12.slot_ref, bf16[64,5,16,256]{3,2,1,0:T(8,128)(2,1)S(1)} %all_to_all.10.mine_ref, ...), custom_call_target="tpu_custom_call" | custom-call | flops 4294967296 | bytes 9437184 | tf_op jit(solution)/shard_map/visibility/pallas_call | solution.py:228
  91.1 105.3 %all_to_all.11 = bf16[256,2,32,128]{3,2,1,0:T(8,128)(2,1)S(1)} all-to-all(bf16[256,2,32,128]{3,2,1,0:T(8,128)(2,1)S(1)} %bitcast.4), channel_id=1, replica_groups=mesh['stn'=64,'band'=4] {'stn','band'}, dimensions={0} | all-to-all | bytes 8388608 | tf_op jit(solution)/shard_map/all_to_all | solution.py:241
  196.4 2.7 %place.1 = bf16[64,4,2,32,128]{4,3,2,1,0:T(8,128)(2,1)} custom-call(s32[4,64]{1,0:T(4,128)S(1)} %get-tuple-element.9.place_ref, bf16[32,2,4,2,32,128]{5,4,3,2,1,0:T(8,128)(2,1)S(1)} %bitcast.3), custom_call_target="tpu_custom_call" | custom-call | bytes 8388608 | tf_op jit(solution)/shard_map/place/pallas_call | solution.py:243
Async XLA Ops:
  3.2 74.0 %copy-start = (s32[4,64]{1,0:T(4,128)S(1)}, s32[4,64]{1,0:T(4,128)}, u32[]{:S(2)}) copy-start(s32[4,64]{1,0:T(4,128)} %count_ref.3) | copy-start | bytes 3076
  3.2 74.0 %copy-start.1 = (s32[4,128]{1,0:T(4,128)S(1)}, s32[4,128]{1,0:T(4,128)}, u32[]{:S(2)}) copy-start(s32[4,128]{1,0:T(4,128)} %level_ref.1) | copy-start | bytes 6148
  3.2 74.0 %copy-start.2 = (f32[64]{0:T(128)S(1)}, f32[64]{0:T(128)}, u32[]{:S(2)}) copy-start(f32[64]{0:T(128)} %gain_ref.1) | copy-start | bytes 772
  3.2 74.0 %copy-start.3 = (s32[64]{0:T(128)S(1)}, s32[64]{0:T(128)}, u32[]{:S(2)}) copy-start(s32[64]{0:T(128)} %order_ref.1) | copy-start | bytes 772
  76.8 8.5 %collective-permute-start = (bf16[64,5,16,256]{3,2,1,0:T(8,128)(2,1)S(1)}, bf16[64,5,16,256]{3,2,1,0:T(8,128)(2,1)S(1)}, u32[]{:S(2)}, u32[]{:S(2)}) collective-permute-start(bf16[64,5,16,256]{3,2,1,0:T(8,128)(2,1)S(1)} %all_to_all.10.mine_ref), channel_id=1, source_target_pairs={{0,4},{4,0},{8,12},{12,8},{16,20},{20,16},{24,28},{28,24},{32,36},... | collective-permute-start | bytes 7864328 | tf_op jit(solution)/shard_map/ppermute | solution.py:227

commit v4 on v3

--- a/solution.py
+++ b/solution.py
@@ -59,12 +59,21 @@
         chip = jnp.where(large, place, GROUPS - 1 - place)
         base = jnp.where(large, SLOTS - size, 0)
 
+        alone = jnp.where(large, size - 1, size)
+
         def send(i):
-            pltpu.make_async_copy(held.at[:, start + i], send_ref.at[pl.ds(2 * chip, 2), base + i], sent).start()
-
-        send(0)
-        for i in range(1, MOST):
-            pl.when(i < size)(functools.partial(send, i))
+            slot = base + i
+            target = send_ref.at[2 * chip + (slot >> 1), pl.ds(2 * (slot & 1), 2)]
+            pltpu.make_async_copy(held.at[:, start + i], target, sent).start()
+
+        for i in range(MOST - 1):
+            pl.when(i < alone)(functools.partial(send, i))
+
+        @pl.when(large)
+        def _():
+            target = send_ref.at[pl.ds(2 * chip, 2), SLOTS - 1]
+            pltpu.make_async_copy(held.at[:, start + size - 1], target, sent).start()
+
         return places, start + size
 
     lax.fori_loop(0, GROUPS, one_group, (places, jnp.int32(0)), unroll=4)
@@ -116,55 +125,60 @@
     lax.fori_loop(0, GROUPS, one_slot, 0, unroll=8)
 
 
-def visibility_kernel(meta_ref, weight_ref, slot_ref, mine_ref, other_ref, out_ref, total):
+def add_products(total, u_ref, v_ref, weight, imaginary):
+    stations = u_ref.shape[1]
+    tall = SUPER // stations
+    for row in range(0, SP, SUPER):
+        r = row // stations
+        u = u_ref[r : r + tall].reshape(SUPER, TIME)
+        v = v_ref[r : r + tall].reshape(SUPER, TIME)
+        right = u_ref[r:].reshape(SP - row, TIME), v_ref[r:].reshape(SP - row, TIME)
+        total[row : row + SUPER, row:] += weight * lax.dot_general(
+            jnp.concatenate((v, -u) if imaginary else (u, v), 1),
+            jnp.concatenate(right, 1),
+            (((1,), (1,)), ((), ())),
+            preferred_element_type=jnp.float32,
+        )
+
+
+def add_pair(core, owner, meta_ref, weight_ref, got_ref, totals):
+    def one_slot(j, carry):
+        t = 2 * owner + j
+        large = t >= SLOTS - meta_ref[1]
+        used = large | (t < meta_ref[0])
+        total = totals.at[large.astype(jnp.int32)]
+        for imaginary in range(2):
+
+            @pl.when(used & (core == imaginary))
+            def _():
+                add_products(total, got_ref.at[:, 2 * j], got_ref.at[:, 2 * j + 1], weight_ref[t], imaginary)
+
+        return carry
+
+    lax.fori_loop(0, 2, one_slot, 0)
+
+
+def early_kernel(meta_ref, weight_ref, mine_ref, totals):
+    core = meta_ref[4]
+    totals[...] = jnp.zeros_like(totals)
+    add_pair(core, core, meta_ref, weight_ref, mine_ref, totals)
+
+
+def visibility_kernel(meta_ref, weight_ref, slot_ref, mine_ref, other_ref, _, out_ref, totals):
     core = meta_ref[4]
     sign = (1 - 2 * core).astype(jnp.float32)
-    stations = mine_ref.shape[2]
-    tall = SUPER // stations
+    add_pair(core, 1 - core, meta_ref, weight_ref, other_ref, totals)
+    last = SLOTS - 1
+    parts = mine_ref.at[:, last], other_ref.at[:, last]
+    for imaginary in range(2):
+
+        @pl.when(core == imaginary)
+        def _():
+            real, imag = parts[::-1] if imaginary else parts
+            add_products(totals.at[1], real, imag, weight_ref[last], imaginary)
 
     for large in range(2):
-        size = meta_ref[large]
-        base = SLOTS - size if large else 0
-
-        def one_channel(i, carry):
-            t = base + i
-            weight = weight_ref[t]
-
-            def products(first, imaginary):
-                for row in range(0, SP, SUPER):
-                    r = row // stations
-                    u = mine_ref[r : r + tall, t].reshape(SUPER, TIME)
-                    v = other_ref[r : r + tall, t].reshape(SUPER, TIME)
-                    all_u = mine_ref[r:, t].reshape(SP - row, TIME)
-                    all_v = other_ref[r:, t].reshape(SP - row, TIME)
-                    if imaginary:
-                        left, right = (u, -v), (all_v, all_u)
-                    else:
-                        left, right = (u, v), (all_u, all_v)
-                    part = weight * lax.dot_general(
-                        jnp.concatenate(left, 1),
-                        jnp.concatenate(right, 1),
-                        (((1,), (1,)), ((), ())),
-                        preferred_element_type=jnp.float32,
-                    )
-                    if first:
-                        total[row : row + SUPER, row:] = part
-                    else:
-                        total[row : row + SUPER, row:] += part
-
-            for imaginary in range(2):
-
-                @pl.when((core == imaginary) & (i == 0))
-                def _():
-                    products(True, imaginary)
-
-                @pl.when((core == imaginary) & (i > 0))
-                def _():
-                    products(False, imaginary)
-
-            return carry
-
-        lax.fori_loop(0, size, one_channel, 0)
+        total = totals.at[large]
 
         def store(p, q, block):
             out_ref[slot_ref[SIDE * p + q], :, large] = block.reshape(BANDS, ROWS, BB)
@@ -225,18 +239,28 @@
     )(group_count, levels, bandpass, block_order)
     mine = lax.all_to_all(sending, "stn", split_axis=0, concat_axis=0, tiled=True)
     other = lax.ppermute(mine, "stn", [(i, i ^ 1) for i in range(owners)])
-    blocks = pl.pallas_call(
+    totals = pl.pallas_call(
+        early_kernel,
+        out_shape=jax.ShapeDtypeStruct((2, SP, SP), jnp.float32),
+        in_specs=[SMEM, SMEM, VMEM],
+        out_specs=VMEM,
+        cost_estimate=pl.CostEstimate(flops=2 << 30, bytes_accessed=10 << 20, transcendentals=0),
+        compiler_params=pltpu.CompilerParams(vmem_limit_bytes=24 << 20),
+        name="early",
+    )(meta, weights, mine)
+    blocks, _ = pl.pallas_call(
         visibility_kernel,
-        out_shape=jax.ShapeDtypeStruct((GROUPS, BANDS, 2, ROWS, BB), jnp.bfloat16),
-        in_specs=[SMEM, SMEM, SMEM, VMEM, VMEM],
-        out_specs=VMEM,
-        scratch_shapes=[
-            pltpu.VMEM((SP, SP), jnp.float32),
-        ],
+        out_shape=(
+            jax.ShapeDtypeStruct((GROUPS, BANDS, 2, ROWS, BB), jnp.bfloat16),
+            jax.ShapeDtypeStruct(totals.shape, totals.dtype),
+        ),
+        in_specs=[SMEM, SMEM, SMEM, VMEM, VMEM, VMEM],
+        out_specs=(VMEM, VMEM),
+        input_output_aliases={5: 1},
         cost_estimate=pl.CostEstimate(flops=4 << 30, bytes_accessed=9 << 20, transcendentals=0),
         compiler_params=pltpu.CompilerParams(vmem_limit_bytes=24 << 20),
         name="visibility",
-    )(meta, weights, slots, mine, other)
+    )(meta, weights, slots, mine, other, totals)
     blocks = blocks.reshape(GROUPS * BANDS, 2, ROWS, BB)
     got = lax.all_to_all(blocks, ("stn", "band"), split_axis=0, concat_axis=0, tiled=True)
     got = got.reshape(CHIPS, 2, BANDS, 2, ROWS, BB)

time: 202 us -> 204 us (level)
    pallas_call x1 -> x2, Pallas kernels: 5.76 us -> 7 us  [the longest x1 4.07 us: body(): pl.pallas_call(visibility_kernel, out_shape=(jax.ShapeDtypeStruct((GROUPS...]
  transfers between devices with their start and end apart: 1 -> 1, of which waited for: 0 -> 0; matrix products, arithmetic and copies ran while one was open for 0% -> 0% of each run, Pallas kernels for 4% -> 5%
where the time goes in v4:
time: 204 us; the launch traced here: 201 us
  blocking collectives  179 us (88%)
  Pallas kernels  21.5 us (11%)
    all_to_all x1, blocking collectives, body(): lax.all_to_all(blocks, ('stn', 'band'), split_axis=0, concat_axis=0, tile...  105 us
    all_to_all x1, blocking collectives, body(): lax.all_to_all(sending, 'stn', split_axis=0, concat_axis=0, tiled=True)  73.4 us
    pallas_call x1, Pallas kernels, body(): pl.pallas_call(index_kernel, out_shape=(jax.ShapeDtypeStruct((8,), jnp.in...  8.04 us
  transfers between devices with their start and end apart: 1, of which 0 were waited for; matrix products, arithmetic and copies ran while one was open for 0% of the time, Pallas kernels for 5%

profile of v4, /device:TPU:32, one launch (start us, length us, event | category | flops | bytes accessed | tf_op | source)
XLA Modules:
  0.0 200.7 jit_solution(7066549278403089374)
XLA Ops:
  0.0 0.0 copy-start
  0.0 0.0 copy-start.3
  0.0 0.0 copy-start.2
  0.0 0.0 copy-start.1
  0.0 3.8 %build.1 = bf16[64,5,16,256]{3,2,1,0:T(8,128)(2,1)} custom-call(s32[4,64]{1,0:T(4,128)} %count_ref.3, bf16[2,128,16,256]{3,2,1,0:T(8,128)(2,1)} %volt_ref.1), custom_call_target="tpu_custom_call" | custom-call | bytes 5242880 | tf_op jit(solution)/shard_map/build/pallas_call | solution.py:212
  3.8 73.4 %all_to_all.10.mine_ref = bf16[64,5,16,256]{3,2,1,0:T(8,128)(2,1)S(1)} all-to-all(bf16[64,5,16,256]{3,2,1,0:T(8,128)(2,1)} %build.1), channel_id=1, replica_groups=mesh['stn'=64,'band'=4] {'stn'}, dimensions={0} | all-to-all | bytes 5242880 | tf_op jit(solution)/shard_map/all_to_all | solution.py:240
  77.2 0.5 collective-permute-start
  77.6 0.0 copy-done
  77.6 0.0 copy-done.3
  77.6 0.0 copy-done.2
  77.6 0.0 copy-done.1
  77.7 8.0 %index.1 = (s32[8]{0:T(128)S(1)}, f32[8]{0:T(128)S(1)}, s32[64]{0:T(128)S(1)}, s32[4,64]{1,0:T(4,128)S(1)}) custom-call(s32[4,64]{1,0:T(4,128)S(1)} %copy-done, s32[4,128]{1,0:T(4,128)S(1)} %copy-done.1, f32[64]{0:T(128)S(1)} %copy-done.2, s32[64]{0:T(128)S(1)} %copy-done.3), custom_call_target="tpu_custom_call" | custom-call | bytes 8388608 | tf_op jit(solution)/shard_map/index/pallas_call | solution.py:226
  85.7 2.9 %early.1._ = f32[2,1024,1024]{2,1,0:T(8,128)S(1)} custom-call(s32[8]{0:T(128)S(1)} %get-tuple-element.11.meta_ref, f32[8]{0:T(128)S(1)} %get-tuple-element.12.weight_ref, bf16[64,5,16,256]{3,2,1,0:T(8,128)(2,1)S(1)} %all_to_all.10.mine_ref), custom_call_target="tpu_custom_call" | custom-call | flops 2147483648 | bytes 10485760 | tf_op jit(solution)/shard_map/early/pallas_call | solution.py:242
  88.6 0.0 collective-permute-done.other_ref
  88.7 4.1 %visibility.1 = (bf16[64,4,2,32,128]{4,3,2,1,0:T(8,128)(2,1)S(1)}, f32[2,1024,1024]{2,1,0:T(8,128)S(1)}) custom-call(s32[8]{0:T(128)S(1)} %get-tuple-element.11.meta_ref, f32[8]{0:T(128)S(1)} %get-tuple-element.12.weight_ref, s32[64]{0:T(128)S(1)} %get-tuple-element.13.slot_ref, ...), custom_call_target="tpu_custom_call", output_to_operand_aliasing={{1}: (5, {})} | custom-call | flops 4294967296 | bytes 9437184 | tf_op jit(solution)/shard_map/visibility/pallas_call | solution.py:251
  92.7 105.3 %all_to_all.11 = bf16[256,2,32,128]{3,2,1,0:T(8,128)(2,1)S(1)} all-to-all(bf16[256,2,32,128]{3,2,1,0:T(8,128)(2,1)S(1)} %bitcast.4), channel_id=1, replica_groups=mesh['stn'=64,'band'=4] {'stn','band'}, dimensions={0} | all-to-all | bytes 8388608 | tf_op jit(solution)/shard_map/all_to_all | solution.py:265
  198.0 2.7 %place.1 = bf16[64,4,2,32,128]{4,3,2,1,0:T(8,128)(2,1)} custom-call(s32[4,64]{1,0:T(4,128)S(1)} %get-tuple-element.10.place_ref, bf16[32,2,4,2,32,128]{5,4,3,2,1,0:T(8,128)(2,1)S(1)} %bitcast.3), custom_call_target="tpu_custom_call" | custom-call | bytes 8388608 | tf_op jit(solution)/shard_map/place/pallas_call | solution.py:267
Async XLA Ops:
  0.0 77.6 %copy-start = (s32[4,64]{1,0:T(4,128)S(1)}, s32[4,64]{1,0:T(4,128)}, u32[]{:S(2)}) copy-start(s32[4,64]{1,0:T(4,128)} %count_ref.3) | copy-start | bytes 3076
  0.0 77.6 %copy-start.3 = (s32[64]{0:T(128)S(1)}, s32[64]{0:T(128)}, u32[]{:S(2)}) copy-start(s32[64]{0:T(128)} %order_ref.1) | copy-start | bytes 772
  0.0 77.6 %copy-start.2 = (f32[64]{0:T(128)S(1)}, f32[64]{0:T(128)}, u32[]{:S(2)}) copy-start(f32[64]{0:T(128)} %gain_ref.1) | copy-start | bytes 772
  0.0 77.6 %copy-start.1 = (s32[4,128]{1,0:T(4,128)S(1)}, s32[4,128]{1,0:T(4,128)}, u32[]{:S(2)}) copy-start(s32[4,128]{1,0:T(4,128)} %level_ref.1) | copy-start | bytes 6148
  77.2 11.5 %collective-permute-start = (bf16[64,5,16,256]{3,2,1,0:T(8,128)(2,1)S(1)}, bf16[64,5,16,256]{3,2,1,0:T(8,128)(2,1)S(1)}, u32[]{:S(2)}, u32[]{:S(2)}) collective-permute-start(bf16[64,5,16,256]{3,2,1,0:T(8,128)(2,1)S(1)} %all_to_all.10.mine_ref), channel_id=1, source_target_pairs={{0,4},{4,0},{8,12},{12,8},{16,20},{20,16},{24,28},{28,24},{32,36},... | collective-permute-start | bytes 7864328 | tf_op jit(solution)/shard_map/ppermute | solution.py:241

commit v5 on v4

--- a/solution.py
+++ b/solution.py
@@ -59,21 +59,13 @@
         chip = jnp.where(large, place, GROUPS - 1 - place)
         base = jnp.where(large, SLOTS - size, 0)
 
-        alone = jnp.where(large, size - 1, size)
-
         def send(i):
-            slot = base + i
-            target = send_ref.at[2 * chip + (slot >> 1), pl.ds(2 * (slot & 1), 2)]
+            target = send_ref.at[chip, pl.ds(2 * (base + i), 2)]
             pltpu.make_async_copy(held.at[:, start + i], target, sent).start()
 
-        for i in range(MOST - 1):
-            pl.when(i < alone)(functools.partial(send, i))
-
-        @pl.when(large)
-        def _():
-            target = send_ref.at[pl.ds(2 * chip, 2), SLOTS - 1]
-            pltpu.make_async_copy(held.at[:, start + size - 1], target, sent).start()
-
+        send(0)
+        for i in range(1, MOST):
+            pl.when(i < size)(functools.partial(send, i))
         return places, start + size
 
     lax.fori_loop(0, GROUPS, one_group, (places, jnp.int32(0)), unroll=4)
@@ -143,7 +135,8 @@
 
 def add_pair(core, owner, meta_ref, weight_ref, got_ref, totals):
     def one_slot(j, carry):
-        t = 2 * owner + j
+        t = 3 * owner + j
+        unit = owner + 2 * j
         large = t >= SLOTS - meta_ref[1]
         used = large | (t < meta_ref[0])
         total = totals.at[large.astype(jnp.int32)]
@@ -151,7 +144,7 @@
 
             @pl.when(used & (core == imaginary))
             def _():
-                add_products(total, got_ref.at[:, 2 * j], got_ref.at[:, 2 * j + 1], weight_ref[t], imaginary)
+                add_products(total, got_ref.at[:, unit], got_ref.at[:, unit + 1], weight_ref[t], imaginary)
 
         return carry
 
@@ -168,14 +161,15 @@
     core = meta_ref[4]
     sign = (1 - 2 * core).astype(jnp.float32)
     add_pair(core, 1 - core, meta_ref, weight_ref, other_ref, totals)
-    last = SLOTS - 1
-    parts = mine_ref.at[:, last], other_ref.at[:, last]
+    shared = 2
     for imaginary in range(2):
 
-        @pl.when(core == imaginary)
+        @pl.when((core == imaginary) & (shared >= SLOTS - meta_ref[1]))
         def _():
-            real, imag = parts[::-1] if imaginary else parts
-            add_products(totals.at[1], real, imag, weight_ref[last], imaginary)
+            first_ref, second_ref = (other_ref, mine_ref) if imaginary else (mine_ref, other_ref)
+            add_products(
+                totals.at[1], first_ref.at[:, SLOTS - 1], second_ref.at[:, 0], weight_ref[shared], imaginary
+            )
 
     for large in range(2):
         total = totals.at[large]
@@ -211,7 +205,7 @@
     owners = lax.axis_size("stn")
     sending = pl.pallas_call(
         build_kernel,
-        out_shape=jax.ShapeDtypeStruct((owners, SLOTS, stations, samples), jnp.bfloat16),
+        out_shape=jax.ShapeDtypeStruct((CHIPS, 2 * SLOTS, stations, samples), jnp.bfloat16),
         in_specs=[ANY, ANY],
         out_specs=ANY,
         scratch_shapes=[
@@ -237,6 +231,7 @@
         compiler_params=pltpu.CompilerParams(vmem_limit_bytes=2 << 20),
         name="index",
     )(group_count, levels, bandpass, block_order)
+    sending = sending.reshape(owners, SLOTS, stations, samples)
     mine = lax.all_to_all(sending, "stn", split_axis=0, concat_axis=0, tiled=True)
     other = lax.ppermute(mine, "stn", [(i, i ^ 1) for i in range(owners)])
     totals = pl.pallas_call(

time: 204 us -> 203 us (level)
  no operation moved by 1% of the time
where the time goes in v5:
time: 203 us; the launch traced here: 200 us
  blocking collectives  179 us (88%)
  Pallas kernels  21 us (10%)
    all_to_all x1, blocking collectives, body(): lax.all_to_all(blocks, ('stn', 'band'), split_axis=0, concat_axis=0, tile...  105 us
    all_to_all x1, blocking collectives, body(): lax.all_to_all(sending, 'stn', split_axis=0, concat_axis=0, tiled=True)  73.4 us
    pallas_call x1, Pallas kernels, body(): pl.pallas_call(index_kernel, out_shape=(jax.ShapeDtypeStruct((8,), jnp.in...  8.04 us
    pallas_call x1, Pallas kernels, body(): pl.pallas_call(visibility_kernel, out_shape=(jax.ShapeDtypeStruct((GROUPS...  4.18 us
  transfers between devices with their start and end apart: 1, of which 0 were waited for; matrix products, arithmetic and copies ran while one was open for 0% of the time, Pallas kernels for 5%

profile of v5, /device:TPU:32, one launch (start us, length us, event | category | flops | bytes accessed | tf_op | source)
XLA Modules:
  0.0 200.2 jit_solution(7753613186865183168)
XLA Ops:
  0.0 0.0 copy-start
  0.0 0.0 copy-start.3
  0.0 0.0 copy-start.2
  0.0 0.0 copy-start.1
  0.0 3.2 %build.1 = bf16[32,10,16,256]{3,2,1,0:T(8,128)(2,1)} custom-call(s32[4,64]{1,0:T(4,128)} %count_ref.3, bf16[2,128,16,256]{3,2,1,0:T(8,128)(2,1)} %volt_ref.1), custom_call_target="tpu_custom_call" | custom-call | bytes 5242880 | tf_op jit(solution)/shard_map/build/pallas_call | solution.py:206
  3.3 73.4 %all_to_all.10.mine_ref = bf16[64,5,16,256]{3,2,1,0:T(8,128)(2,1)S(1)} all-to-all(bf16[64,5,16,256]{3,2,1,0:T(8,128)(2,1)} %bitcast.6), channel_id=1, replica_groups=mesh['stn'=64,'band'=4] {'stn'}, dimensions={0} | all-to-all | bytes 5242880 | tf_op jit(solution)/shard_map/all_to_all | solution.py:235
  76.6 0.5 collective-permute-start
  77.1 0.0 copy-done
  77.1 0.0 copy-done.3
  77.1 0.0 copy-done.2
  77.1 0.0 copy-done.1
  77.1 8.0 %index.1 = (s32[8]{0:T(128)S(1)}, f32[8]{0:T(128)S(1)}, s32[64]{0:T(128)S(1)}, s32[4,64]{1,0:T(4,128)S(1)}) custom-call(s32[4,64]{1,0:T(4,128)S(1)} %copy-done, s32[4,128]{1,0:T(4,128)S(1)} %copy-done.1, f32[64]{0:T(128)S(1)} %copy-done.2, s32[64]{0:T(128)S(1)} %copy-done.3), custom_call_target="tpu_custom_call" | custom-call | bytes 8388608 | tf_op jit(solution)/shard_map/index/pallas_call | solution.py:220
  85.2 2.9 %early.1._ = f32[2,1024,1024]{2,1,0:T(8,128)S(1)} custom-call(s32[8]{0:T(128)S(1)} %get-tuple-element.11.meta_ref, f32[8]{0:T(128)S(1)} %get-tuple-element.12.weight_ref, bf16[64,5,16,256]{3,2,1,0:T(8,128)(2,1)S(1)} %all_to_all.10.mine_ref), custom_call_target="tpu_custom_call" | custom-call | flops 2147483648 | bytes 10485760 | tf_op jit(solution)/shard_map/early/pallas_call | solution.py:237
  88.0 0.0 collective-permute-done.other_ref
  88.1 4.2 %visibility.1 = (bf16[64,4,2,32,128]{4,3,2,1,0:T(8,128)(2,1)S(1)}, f32[2,1024,1024]{2,1,0:T(8,128)S(1)}) custom-call(s32[8]{0:T(128)S(1)} %get-tuple-element.11.meta_ref, f32[8]{0:T(128)S(1)} %get-tuple-element.12.weight_ref, s32[64]{0:T(128)S(1)} %get-tuple-element.13.slot_ref, ...), custom_call_target="tpu_custom_call", output_to_operand_aliasing={{1}: (5, {})} | custom-call | flops 4294967296 | bytes 9437184 | tf_op jit(solution)/shard_map/visibility/pallas_call | solution.py:246
  92.2 105.3 %all_to_all.11 = bf16[256,2,32,128]{3,2,1,0:T(8,128)(2,1)S(1)} all-to-all(bf16[256,2,32,128]{3,2,1,0:T(8,128)(2,1)S(1)} %bitcast.5), channel_id=1, replica_groups=mesh['stn'=64,'band'=4] {'stn','band'}, dimensions={0} | all-to-all | bytes 8388608 | tf_op jit(solution)/shard_map/all_to_all | solution.py:260
  197.5 2.7 %place.1 = bf16[64,4,2,32,128]{4,3,2,1,0:T(8,128)(2,1)} custom-call(s32[4,64]{1,0:T(4,128)S(1)} %get-tuple-element.10.place_ref, bf16[32,2,4,2,32,128]{5,4,3,2,1,0:T(8,128)(2,1)S(1)} %bitcast.4), custom_call_target="tpu_custom_call" | custom-call | bytes 8388608 | tf_op jit(solution)/shard_map/place/pallas_call | solution.py:262
Async XLA Ops:
  0.0 77.1 %copy-start = (s32[4,64]{1,0:T(4,128)S(1)}, s32[4,64]{1,0:T(4,128)}, u32[]{:S(2)}) copy-start(s32[4,64]{1,0:T(4,128)} %count_ref.3) | copy-start | bytes 3076
  0.0 77.1 %copy-start.3 = (s32[64]{0:T(128)S(1)}, s32[64]{0:T(128)}, u32[]{:S(2)}) copy-start(s32[64]{0:T(128)} %order_ref.1) | copy-start | bytes 772
  0.0 77.1 %copy-start.2 = (f32[64]{0:T(128)S(1)}, f32[64]{0:T(128)}, u32[]{:S(2)}) copy-start(f32[64]{0:T(128)} %gain_ref.1) | copy-start | bytes 772
  0.0 77.1 %copy-start.1 = (s32[4,128]{1,0:T(4,128)S(1)}, s32[4,128]{1,0:T(4,128)}, u32[]{:S(2)}) copy-start(s32[4,128]{1,0:T(4,128)} %level_ref.1) | copy-start | bytes 6148
  76.6 11.4 %collective-permute-start = (bf16[64,5,16,256]{3,2,1,0:T(8,128)(2,1)S(1)}, bf16[64,5,16,256]{3,2,1,0:T(8,128)(2,1)S(1)}, u32[]{:S(2)}, u32[]{:S(2)}) collective-permute-start(bf16[64,5,16,256]{3,2,1,0:T(8,128)(2,1)S(1)} %all_to_all.10.mine_ref), channel_id=1, source_target_pairs={{0,4},{4,0},{8,12},{12,8},{16,20},{20,16},{24,28},{28,24},{32,36},... | collective-permute-start | bytes 7864328 | tf_op jit(solution)/shard_map/ppermute | solution.py:236

commit v6 on v5

--- a/solution.py
+++ b/solution.py
@@ -161,17 +161,8 @@
     core = meta_ref[4]
     sign = (1 - 2 * core).astype(jnp.float32)
     add_pair(core, 1 - core, meta_ref, weight_ref, other_ref, totals)
-    shared = 2
-    for imaginary in range(2):
-
-        @pl.when((core == imaginary) & (shared >= SLOTS - meta_ref[1]))
-        def _():
-            first_ref, second_ref = (other_ref, mine_ref) if imaginary else (mine_ref, other_ref)
-            add_products(
-                totals.at[1], first_ref.at[:, SLOTS - 1], second_ref.at[:, 0], weight_ref[shared], imaginary
-            )
-
-    for large in range(2):
+
+    def finish(large, sign):
         total = totals.at[large]
 
         def store(p, q, block):
@@ -185,18 +176,35 @@
                 if q // per > p // per:
                     store(q, p, (sign * block).astype(jnp.bfloat16).T)
 
+    shared = 2
+    held = shared >= SLOTS - meta_ref[1]
+    for imaginary in range(2):
+
+        @pl.when((core == imaginary) & held)
+        def _():
+            first_ref, second_ref = (other_ref, mine_ref) if imaginary else (mine_ref, other_ref)
+            add_products(
+                totals.at[1], first_ref.at[:, SLOTS - 1], second_ref.at[:, 0], weight_ref[shared], imaginary
+            )
+            finish(0, -1.0 if imaginary else 1.0)
+
+    @pl.when(jnp.logical_not(held))
+    def _():
+        finish(0, sign)
+
+    finish(1, sign)
+
 
 def place_kernel(place_ref, got_ref, out_ref, landed):
-    for band in range(BANDS):
-
-        def one_group(g, carry):
+    def one_group(g, carry):
+        for band in range(BANDS):
             place = place_ref[band, g]
             large = (place < HALF).astype(jnp.int32)
             chip = jnp.where(place < HALF, place, GROUPS - 1 - place)
             pltpu.make_async_copy(got_ref.at[chip, :, band, large], out_ref.at[g, band], landed).start()
-            return carry
-
-        lax.fori_loop(0, GROUPS, one_group, 0, unroll=8)
+        return carry
+
+    lax.fori_loop(0, GROUPS, one_group, 0, unroll=4)
     pltpu.make_async_copy(out_ref, out_ref, landed).wait()
 
 

time: 203 us -> 203 us (level)
  no operation moved by 1% of the time
where the time goes in v6:
time: 203 us; the launch traced here: 200 us
  blocking collectives  179 us (88%)
  Pallas kernels  20.5 us (10%)
    all_to_all x1, blocking collectives, body(): lax.all_to_all(blocks, ('stn', 'band'), split_axis=0, concat_axis=0, tile...  105 us
    all_to_all x1, blocking collectives, body(): lax.all_to_all(sending, 'stn', split_axis=0, concat_axis=0, tiled=True)  73.4 us
    pallas_call x1, Pallas kernels, body(): pl.pallas_call(index_kernel, out_shape=(jax.ShapeDtypeStruct((8,), jnp.in...  8.04 us
  transfers between devices with their start and end apart: 1, of which 0 were waited for; matrix products, arithmetic and copies ran while one was open for 0% of the time, Pallas kernels for 5%

profile of v6, /device:TPU:32, one launch (start us, length us, event | category | flops | bytes accessed | tf_op | source)
XLA Modules:
  0.0 199.8 jit_solution(4371687275161604359)
XLA Ops:
  0.0 0.0 copy-start
  0.0 0.0 copy-start.3
  0.0 0.0 copy-start.2
  0.0 0.0 copy-start.1
  0.0 3.2 %build.1 = bf16[32,10,16,256]{3,2,1,0:T(8,128)(2,1)} custom-call(s32[4,64]{1,0:T(4,128)} %count_ref.3, bf16[2,128,16,256]{3,2,1,0:T(8,128)(2,1)} %volt_ref.1), custom_call_target="tpu_custom_call" | custom-call | bytes 5242880 | tf_op jit(solution)/shard_map/build/pallas_call | solution.py:214
  3.3 73.4 %all_to_all.10.mine_ref = bf16[64,5,16,256]{3,2,1,0:T(8,128)(2,1)S(1)} all-to-all(bf16[64,5,16,256]{3,2,1,0:T(8,128)(2,1)} %bitcast.6), channel_id=1, replica_groups=mesh['stn'=64,'band'=4] {'stn'}, dimensions={0} | all-to-all | bytes 5242880 | tf_op jit(solution)/shard_map/all_to_all | solution.py:243
  76.6 0.5 collective-permute-start
  77.1 0.0 copy-done
  77.1 0.0 copy-done.3
  77.1 0.0 copy-done.2
  77.1 0.0 copy-done.1
  77.1 8.0 %index.1 = (s32[8]{0:T(128)S(1)}, f32[8]{0:T(128)S(1)}, s32[64]{0:T(128)S(1)}, s32[4,64]{1,0:T(4,128)S(1)}) custom-call(s32[4,64]{1,0:T(4,128)S(1)} %copy-done, s32[4,128]{1,0:T(4,128)S(1)} %copy-done.1, f32[64]{0:T(128)S(1)} %copy-done.2, s32[64]{0:T(128)S(1)} %copy-done.3), custom_call_target="tpu_custom_call" | custom-call | bytes 8388608 | tf_op jit(solution)/shard_map/index/pallas_call | solution.py:228
  85.2 2.9 %early.1._ = f32[2,1024,1024]{2,1,0:T(8,128)S(1)} custom-call(s32[8]{0:T(128)S(1)} %get-tuple-element.11.meta_ref, f32[8]{0:T(128)S(1)} %get-tuple-element.12.weight_ref, bf16[64,5,16,256]{3,2,1,0:T(8,128)(2,1)S(1)} %all_to_all.10.mine_ref), custom_call_target="tpu_custom_call" | custom-call | flops 2147483648 | bytes 10485760 | tf_op jit(solution)/shard_map/early/pallas_call | solution.py:245
  88.0 0.0 collective-permute-done.other_ref
  88.1 3.9 %visibility.1 = (bf16[64,4,2,32,128]{4,3,2,1,0:T(8,128)(2,1)S(1)}, f32[2,1024,1024]{2,1,0:T(8,128)S(1)}) custom-call(s32[8]{0:T(128)S(1)} %get-tuple-element.11.meta_ref, f32[8]{0:T(128)S(1)} %get-tuple-element.12.weight_ref, s32[64]{0:T(128)S(1)} %get-tuple-element.13.slot_ref, ...), custom_call_target="tpu_custom_call", output_to_operand_aliasing={{1}: (5, {})} | custom-call | flops 4294967296 | bytes 9437184 | tf_op jit(solution)/shard_map/visibility/pallas_call | solution.py:254
  91.9 105.4 %all_to_all.11 = bf16[256,2,32,128]{3,2,1,0:T(8,128)(2,1)S(1)} all-to-all(bf16[256,2,32,128]{3,2,1,0:T(8,128)(2,1)S(1)} %bitcast.5), channel_id=1, replica_groups=mesh['stn'=64,'band'=4] {'stn','band'}, dimensions={0} | all-to-all | bytes 8388608 | tf_op jit(solution)/shard_map/all_to_all | solution.py:268
  197.3 2.5 %place.1 = bf16[64,4,2,32,128]{4,3,2,1,0:T(8,128)(2,1)} custom-call(s32[4,64]{1,0:T(4,128)S(1)} %get-tuple-element.10.place_ref, bf16[32,2,4,2,32,128]{5,4,3,2,1,0:T(8,128)(2,1)S(1)} %bitcast.4), custom_call_target="tpu_custom_call" | custom-call | bytes 8388608 | tf_op jit(solution)/shard_map/place/pallas_call | solution.py:270
Async XLA Ops:
  0.0 77.1 %copy-start = (s32[4,64]{1,0:T(4,128)S(1)}, s32[4,64]{1,0:T(4,128)}, u32[]{:S(2)}) copy-start(s32[4,64]{1,0:T(4,128)} %count_ref.3) | copy-start | bytes 3076
  0.0 77.1 %copy-start.3 = (s32[64]{0:T(128)S(1)}, s32[64]{0:T(128)}, u32[]{:S(2)}) copy-start(s32[64]{0:T(128)} %order_ref.1) | copy-start | bytes 772
  0.0 77.1 %copy-start.2 = (f32[64]{0:T(128)S(1)}, f32[64]{0:T(128)}, u32[]{:S(2)}) copy-start(f32[64]{0:T(128)} %gain_ref.1) | copy-start | bytes 772
  0.0 77.1 %copy-start.1 = (s32[4,128]{1,0:T(4,128)S(1)}, s32[4,128]{1,0:T(4,128)}, u32[]{:S(2)}) copy-start(s32[4,128]{1,0:T(4,128)} %level_ref.1) | copy-start | bytes 6148
  76.6 11.4 %collective-permute-start = (bf16[64,5,16,256]{3,2,1,0:T(8,128)(2,1)S(1)}, bf16[64,5,16,256]{3,2,1,0:T(8,128)(2,1)S(1)}, u32[]{:S(2)}, u32[]{:S(2)}) collective-permute-start(bf16[64,5,16,256]{3,2,1,0:T(8,128)(2,1)S(1)} %all_to_all.10.mine_ref), channel_id=1, source_target_pairs={{0,4},{4,0},{8,12},{12,8},{16,20},{20,16},{24,28},{28,24},{32,36},... | collective-permute-start | bytes 7864328 | tf_op jit(solution)/shard_map/ppermute | solution.py:244

commit v7 on v6

--- a/solution.py
+++ b/solution.py
@@ -166,7 +166,7 @@
         total = totals.at[large]
 
         def store(p, q, block):
-            out_ref[slot_ref[SIDE * p + q], :, large] = block.reshape(BANDS, ROWS, BB)
+            out_ref[:, slot_ref[SIDE * p + q], large] = block.reshape(BANDS, ROWS, BB)
 
         per = SUPER // BB
         for p in range(SIDE):
@@ -201,7 +201,7 @@
             place = place_ref[band, g]
             large = (place < HALF).astype(jnp.int32)
             chip = jnp.where(place < HALF, place, GROUPS - 1 - place)
-            pltpu.make_async_copy(got_ref.at[chip, :, band, large], out_ref.at[g, band], landed).start()
+            pltpu.make_async_copy(got_ref.at[band, chip, :, large], out_ref.at[g, band], landed).start()
         return carry
 
     lax.fori_loop(0, GROUPS, one_group, 0, unroll=4)
@@ -254,7 +254,7 @@
     blocks, _ = pl.pallas_call(
         visibility_kernel,
         out_shape=(
-            jax.ShapeDtypeStruct((GROUPS, BANDS, 2, ROWS, BB), jnp.bfloat16),
+            jax.ShapeDtypeStruct((BANDS, GROUPS, 2, ROWS, BB), jnp.bfloat16),
             jax.ShapeDtypeStruct(totals.shape, totals.dtype),
         ),
         in_specs=[SMEM, SMEM, SMEM, VMEM, VMEM, VMEM],
@@ -265,8 +265,8 @@
         name="visibility",
     )(meta, weights, slots, mine, other, totals)
     blocks = blocks.reshape(GROUPS * BANDS, 2, ROWS, BB)
-    got = lax.all_to_all(blocks, ("stn", "band"), split_axis=0, concat_axis=0, tiled=True)
-    got = got.reshape(CHIPS, 2, BANDS, 2, ROWS, BB)
+    got = lax.all_to_all(blocks, ("band", "stn"), split_axis=0, concat_axis=0, tiled=True)
+    got = got.reshape(BANDS, CHIPS, 2, 2, ROWS, BB)
     out = pl.pallas_call(
         place_kernel,
         out_shape=jax.ShapeDtypeStruct((GROUPS, BANDS, 2, ROWS, BB), jnp.bfloat16),

time: 203 us -> 203 us (level)
  no operation moved by 1% of the time
where the time goes in v7:
time: 203 us; the launch traced here: 200 us
  blocking collectives  179 us (88%)
  Pallas kernels  20.5 us (10%)
    all_to_all x1, blocking collectives, body(): lax.all_to_all(blocks, ('band', 'stn'), split_axis=0, concat_axis=0, tile...  106 us
    all_to_all x1, blocking collectives, body(): lax.all_to_all(sending, 'stn', split_axis=0, concat_axis=0, tiled=True)  73.4 us
    pallas_call x1, Pallas kernels, body(): pl.pallas_call(index_kernel, out_shape=(jax.ShapeDtypeStruct((8,), jnp.in...  8.04 us
  transfers between devices with their start and end apart: 1, of which 0 were waited for; matrix products, arithmetic and copies ran while one was open for 0% of the time, Pallas kernels for 5%

profile of v7, /device:TPU:32, one launch (start us, length us, event | category | flops | bytes accessed | tf_op | source)
XLA Modules:
  0.0 200.1 jit_solution(11940663461782547178)
XLA Ops:
  0.0 0.0 copy-start
  0.0 0.0 copy-start.3
  0.0 0.0 copy-start.2
  0.0 0.0 copy-start.1
  0.0 3.2 %build.1 = bf16[32,10,16,256]{3,2,1,0:T(8,128)(2,1)} custom-call(s32[4,64]{1,0:T(4,128)} %count_ref.3, bf16[2,128,16,256]{3,2,1,0:T(8,128)(2,1)} %volt_ref.1), custom_call_target="tpu_custom_call" | custom-call | bytes 5242880 | tf_op jit(solution)/shard_map/build/pallas_call | solution.py:214
  3.3 73.4 %all_to_all.10.mine_ref = bf16[64,5,16,256]{3,2,1,0:T(8,128)(2,1)S(1)} all-to-all(bf16[64,5,16,256]{3,2,1,0:T(8,128)(2,1)} %bitcast.6), channel_id=1, replica_groups=mesh['stn'=64,'band'=4] {'stn'}, dimensions={0} | all-to-all | bytes 5242880 | tf_op jit(solution)/shard_map/all_to_all | solution.py:243
  76.6 0.5 collective-permute-start
  77.1 0.0 copy-done
  77.1 0.0 copy-done.3
  77.1 0.0 copy-done.2
  77.1 0.0 copy-done.1
  77.1 8.0 %index.1 = (s32[8]{0:T(128)S(1)}, f32[8]{0:T(128)S(1)}, s32[64]{0:T(128)S(1)}, s32[4,64]{1,0:T(4,128)S(1)}) custom-call(s32[4,64]{1,0:T(4,128)S(1)} %copy-done, s32[4,128]{1,0:T(4,128)S(1)} %copy-done.1, f32[64]{0:T(128)S(1)} %copy-done.2, s32[64]{0:T(128)S(1)} %copy-done.3), custom_call_target="tpu_custom_call" | custom-call | bytes 8388608 | tf_op jit(solution)/shard_map/index/pallas_call | solution.py:228
  85.2 2.9 %early.1._ = f32[2,1024,1024]{2,1,0:T(8,128)S(1)} custom-call(s32[8]{0:T(128)S(1)} %get-tuple-element.11.meta_ref, f32[8]{0:T(128)S(1)} %get-tuple-element.12.weight_ref, bf16[64,5,16,256]{3,2,1,0:T(8,128)(2,1)S(1)} %all_to_all.10.mine_ref), custom_call_target="tpu_custom_call" | custom-call | flops 2147483648 | bytes 10485760 | tf_op jit(solution)/shard_map/early/pallas_call | solution.py:245
  88.0 0.0 collective-permute-done.other_ref
  88.1 3.9 %visibility.1 = (bf16[4,64,2,32,128]{4,3,2,1,0:T(8,128)(2,1)S(1)}, f32[2,1024,1024]{2,1,0:T(8,128)S(1)}) custom-call(s32[8]{0:T(128)S(1)} %get-tuple-element.11.meta_ref, f32[8]{0:T(128)S(1)} %get-tuple-element.12.weight_ref, s32[64]{0:T(128)S(1)} %get-tuple-element.13.slot_ref, ...), custom_call_target="tpu_custom_call", output_to_operand_aliasing={{1}: (5, {})} | custom-call | flops 4294967296 | bytes 9437184 | tf_op jit(solution)/shard_map/visibility/pallas_call | solution.py:254
  91.9 105.7 %all_to_all.11 = bf16[256,2,32,128]{3,2,1,0:T(8,128)(2,1)S(1)} all-to-all(bf16[256,2,32,128]{3,2,1,0:T(8,128)(2,1)S(1)} %bitcast.5), channel_id=1, replica_groups=mesh['stn'=64,'band'=4] {'band','stn'}, dimensions={0} | all-to-all | bytes 8388608 | tf_op jit(solution)/shard_map/all_to_all | solution.py:268
  197.6 2.5 %place.1 = bf16[64,4,2,32,128]{4,3,2,1,0:T(8,128)(2,1)} custom-call(s32[4,64]{1,0:T(4,128)S(1)} %get-tuple-element.10.place_ref, bf16[4,32,2,2,32,128]{5,4,3,2,1,0:T(8,128)(2,1)S(1)} %bitcast.4), custom_call_target="tpu_custom_call" | custom-call | bytes 8388608 | tf_op jit(solution)/shard_map/place/pallas_call | solution.py:270
Async XLA Ops:
  0.0 77.1 %copy-start = (s32[4,64]{1,0:T(4,128)S(1)}, s32[4,64]{1,0:T(4,128)}, u32[]{:S(2)}) copy-start(s32[4,64]{1,0:T(4,128)} %count_ref.3) | copy-start | bytes 3076
  0.0 77.1 %copy-start.3 = (s32[64]{0:T(128)S(1)}, s32[64]{0:T(128)}, u32[]{:S(2)}) copy-start(s32[64]{0:T(128)} %order_ref.1) | copy-start | bytes 772
  0.0 77.1 %copy-start.2 = (f32[64]{0:T(128)S(1)}, f32[64]{0:T(128)}, u32[]{:S(2)}) copy-start(f32[64]{0:T(128)} %gain_ref.1) | copy-start | bytes 772
  0.0 77.1 %copy-start.1 = (s32[4,128]{1,0:T(4,128)S(1)}, s32[4,128]{1,0:T(4,128)}, u32[]{:S(2)}) copy-start(s32[4,128]{1,0:T(4,128)} %level_ref.1) | copy-start | bytes 6148
  76.6 11.4 %collective-permute-start = (bf16[64,5,16,256]{3,2,1,0:T(8,128)(2,1)S(1)}, bf16[64,5,16,256]{3,2,1,0:T(8,128)(2,1)S(1)}, u32[]{:S(2)}, u32[]{:S(2)}) collective-permute-start(bf16[64,5,16,256]{3,2,1,0:T(8,128)(2,1)S(1)} %all_to_all.10.mine_ref), channel_id=1, source_target_pairs={{0,4},{4,0},{8,12},{12,8},{16,20},{20,16},{24,28},{28,24},{32,36},... | collective-permute-start | bytes 7864328 | tf_op jit(solution)/shard_map/ppermute | solution.py:244
